TPU v7x, 128 devices: a whole 4x4x4 slice. The times are simulated.
128 devices in a mesh: row: 16 (over y, z), col: 8 (over x, core).
Axes of the slice: x: 4, y: 4, z: 4, core: 2. Of those that a mesh axis runs over, the one named last changes fastest.
Arguments:
- vectors: bfloat16 [12288, 256, 64], P(('row', 'col')), may hold values from -6 to 6
- energies: float32 [12288, 256], P(('row', 'col')), may hold values from 1 to 3
- blocks: bfloat16 [12288, 256, 256], P(('row', 'col')), may hold values from -0.375 to 0.375
- kernel: bfloat16 [16384, 16384], P('row', 'col'), may hold values from -0.00390625 to 0.00390625
- slot_coarse_kpoint: int32 [12288], P(('row', 'col')), may hold values from 0 to 63
- counts: int32 [128], P(('row', 'col')), may hold values from 1 to 96, 8192 in all
Outputs:
- filtered: bfloat16 [12288, 256, 64], P(('row', 'col'))
Inputs may be any that keep to these rules, and one draw needn't show every extreme that they name: Device d (index row * 8 + col in mesh order) holds live fine k-points in its first counts[d] slots; one device has exactly 96.
All inputs are finite; a program needn't handle non-finite values.
Results may differ from a plain program's by a relative error of at most 0.009.
Values may be sent and summed in bfloat16 or wider, within the bound.
A program may use at most 128 MiB of HBM per device.

v0:
```python
import jax
import jax.numpy as jnp
from jax import lax
from jax.sharding import Mesh
from jax.sharding import PartitionSpec as P

ROW_COL = ("row_0", "row_1", "col_0", "col_1")
ROW = ("row_0", "row_1")
COL = ("col_0", "col_1")


def in_blocks(array, dim, length):
    dims = array.shape
    pieces = array.reshape(*dims[:dim], length, dims[dim] // length, *dims[dim + 1 :])
    return jnp.moveaxis(pieces, dim, 0)


def summed_on_arrival(array, axis, dim):
    length = lax.axis_size(axis)
    pieces = lax.all_to_all(in_blocks(array, dim, length), axis, 0, 0, tiled=True)
    return jnp.sum(pieces, axis=0)


def summed_rows(array, axes, dim):
    far, near = axes
    own = summed_on_arrival(in_blocks(array, dim, lax.axis_size(far)), near, dim + 1)
    return jnp.sum(lax.all_to_all(own, far, 0, 0, tiled=True), axis=0)


def from_everyone(array, axis):
    length = lax.axis_size(axis)
    return lax.all_to_all(
        jnp.broadcast_to(array[None], (length, *array.shape)), axis, 0, 0, tiled=True
    )


def in_order(pieces, dim):
    dims = list(pieces.shape[1:])
    dims[dim] *= pieces.shape[0]
    return jnp.moveaxis(pieces, 0, dim).reshape(dims)


def gathered_copies(array, axis, dim):
    pieces = from_everyone(array, axis)
    return in_order(pieces, dim)


def gather_axes(array, axes, dim):
    far, near = axes
    pieces = from_everyone(from_everyone(array, far), near)
    return in_order(pieces.swapaxes(0, 1).reshape(-1, *array.shape), dim)


def collect_coarse(partial_value, n_row, n_col):
    order, width = partial_value.shape
    piece = order // (n_row * n_col)
    arranged = (
        partial_value.reshape(n_col, n_row, piece, width)
        .transpose(1, 0, 2, 3)
        .reshape(order, width)
    )
    mine = summed_rows(arranged, (("row_0", "row_1", "col_0"), "col_1"), 0).astype(jnp.bfloat16)
    return gathered_copies(mine, ROW, 0)


def spread_products(products):
    share = summed_on_arrival(products, COL, 0).astype(jnp.bfloat16)
    return gather_axes(share, (("row_0", "row_1", "col_0"), "col_1"), 0)


def apply_hamiltonian(xb, energies, blocks, kernel, slot_coarse_kpoint, live, onehot, n_row, n_col):
    slots, nbasis, nvecs = xb.shape
    proj = jnp.einsum("sij,sjv->siv", blocks, xb, preferred_element_type=jnp.float32)
    partial_value = jnp.dot(
        onehot, proj.reshape(slots, nbasis * nvecs), precision=lax.Precision.HIGHEST
    )
    order = onehot.shape[0] * nbasis
    columns = collect_coarse(partial_value.reshape(order, nvecs), n_row, n_col)
    products = jnp.dot(kernel, columns, preferred_element_type=jnp.float32)
    whole = spread_products(products).reshape(onehot.shape[0], nbasis, nvecs)
    picked = jnp.take(whole, slot_coarse_kpoint, axis=0)
    back = jnp.einsum("sji,sjv->siv", blocks, picked, preferred_element_type=jnp.float32)
    return energies[:, :, None] * xb.astype(jnp.float32) + live[:, None, None] * back


def local(vectors, energies, blocks, kernel, slot_coarse_kpoint, counts):
    n_row = lax.axis_size(ROW)
    n_col = lax.axis_size(COL)
    slots, nbasis, nvecs = vectors.shape
    order = kernel.shape[0] * n_row
    npoints = order // nbasis
    live = (lax.iota(jnp.int32, slots) < counts[0]).astype(jnp.float32)
    onehot = (lax.iota(jnp.int32, npoints)[:, None] == slot_coarse_kpoint[None, :]).astype(
        jnp.float32
    )
    start = live[:, None, None] * vectors.astype(jnp.float32)
    startb = start.astype(jnp.bfloat16)
    first = (
        apply_hamiltonian(
            startb, energies, blocks, kernel, slot_coarse_kpoint, live, onehot, n_row, n_col
        )
        - 2.0 * start
    ) / 2.0
    firstb = first.astype(jnp.bfloat16)
    second = apply_hamiltonian(
        firstb, energies, blocks, kernel, slot_coarse_kpoint, live, onehot, n_row, n_col
    )
    result = 2.0 * (second - 2.0 * firstb.astype(jnp.float32)) / 2.0 - start
    return result.astype(jnp.bfloat16)


def solution(mesh):
    split = Mesh(mesh.devices.reshape(4, 4, 4, 2), ("row_0", "row_1", "col_0", "col_1"))
    in_specs = (
        P(ROW_COL, None, None),
        P(ROW_COL, None),
        P(ROW_COL, None, None),
        P(ROW, COL),
        P(ROW_COL),
        P(ROW_COL),
    )
    out_specs = P(ROW_COL, None, None)
    return jax.shard_map(local, mesh=split, in_specs=in_specs, out_specs=out_specs, check_vma=False)
```

profile of v0, /device:TPU:1, one launch (start us, length us, event | category | flops | bytes accessed | tf_op | source)
XLA Modules:
  0.0 345.1 jit_solution(7226853961056250346)
XLA Ops:
  1.3 12.1 %fusion.24 = f32[96,256,64]{1,2,0:T(8,128)} fusion(bf16[96,256,256]{2,1,0:T(8,128)(2,1)} %param.10, bf16[96,256,64]{1,2,0:T(8,128)(2,1)} %param.8, f32[96]{0:T(128)S(1)} %get-tuple-element.7), kind=kOutput, calls=%fused_computation.29 | convolution fusion | flops 810024960 | bytes 22020480 | tf_op jit(solution)/shard_map/sij,sjv->siv/dot_general | solution.py:73
  13.5 8.4 %copy.23 = f32[96,256,64]{0,2,1:T(8,128)} copy(f32[96,256,64]{1,2,0:T(8,128)} %fusion.24) | data formatting | bytes 12582912 | tf_op jit(solution)/shard_map/sij,sjv->siv/dot_general | solution.py:73
  21.8 10.6 %fusion.39 = f32[64,16384]{1,0:T(8,128)} fusion(f32[96,16384]{0,1:T(8,128)} %bitcast.77, s32[96]{0:T(128)S(1)} %copy-done.1), kind=kOutput, calls=%fused_computation.45 | convolution fusion | flops 1207965696 | bytes 10486144 | tf_op jit(solution)/shard_map/dot_general | solution.py:74
  32.4 7.4 %reshape_reshape.6 = f32[8,16,128,64]{3,2,1,0:T(8,128)} reshape(f32[64,16384]{1,0:T(8,128)} %fusion.39) | data formatting | bytes 8388608 | tf_op jit(solution)/shard_map/reshape;reshape | solution.py:58
  39.7 6.8 %copy.24 = f32[16,8,128,64]{2,3,1,0:T(8,128)} copy(f32[16,8,128,64]{3,2,0,1:T(8,128)} %bitcast.79) | data formatting | bytes 8388608 | tf_op jit(solution)/shard_map/transpose | solution.py:59
  49.0 9.2 %all_to_all.60 = f32[2,64,128,64]{2,3,1,0:T(8,128)} all-to-all(f32[2,64,128,64]{2,3,1,0:T(8,128)S(1)} %copy.25), channel_id=1, replica_groups=mesh['row_0'=4,'row_1'=4,'col_0'=4,'col_1'=2] {'col_1'}, dimensions={0} | all-to-all | bytes 8388608 | tf_op jit(solution)/shard_map/all_to_all | solution.py:20
  61.0 40.2 %all_to_all.61 = f32[64,128,64]{1,2,0:T(8,128)} all-to-all(f32[64,128,64]{1,2,0:T(8,128)S(1)} %reduce_sum.54), channel_id=1, replica_groups=mesh['row_0'=4,'row_1'=4,'col_0'=4,'col_1'=2] {'row_0','row_1','col_0'}, dimensions={0} | all-to-all | bytes 4194304 | tf_op jit(solution)/shard_map/all_to_all | solution.py:27
  103.0 10.1 %all_to_all.62 = bf16[16,128,64]{1,2,0:T(8,128)(2,1)S(1)} all-to-all(bf16[16,128,64]{1,2,0:T(8,128)(2,1)S(1)} %broadcast_in_dim.21), channel_id=1, replica_groups=mesh['row_0'=4,'row_1'=4,'col_0'=4,'col_1'=2] {'row_0','row_1'}, dimensions={0} | all-to-all | bytes 524288 | tf_op jit(solution)/shard_map/all_to_all | solution.py:32
  116.6 12.7 %all_to_all.63 = f32[8,128,64]{1,2,0:T(8,128)S(1)} all-to-all(f32[8,128,64]{1,2,0:T(8,128)S(1)} %bitcast.83), channel_id=1, replica_groups=mesh['row_0'=4,'row_1'=4,'col_0'=4,'col_1'=2] {'col_0','col_1'}, dimensions={0} | all-to-all | bytes 524288 | tf_op jit(solution)/shard_map/all_to_all | solution.py:20
  135.4 17.4 %all-to-all-done.4 = bf16[64,128,64]{1,2,0:T(8,128)(2,1)S(1)} async-done(((bf16[64,128,64]{1,2,0:T(8,128)(2,1)}), bf16[64,128,64]{1,2,0:T(8,128)(2,1)S(1)}, u32[]{:S(2)}, u32[]{:S(2)}) %all-to-all-start.4) | async-done | bytes 1048608 | tf_op jit(solution)/shard_map/all_to_all | solution.py:32
  153.3 7.5 %all_to_all.64 = bf16[2,64,128,64]{2,3,1,0:T(8,128)(2,1)S(1)} all-to-all(bf16[2,64,128,64]{2,3,1,0:T(8,128)(2,1)S(1)} %broadcast_in_dim.23), channel_id=1, replica_groups=mesh['row_0'=4,'row_1'=4,'col_0'=4,'col_1'=2] {'col_1'}, dimensions={0} | all-to-all | bytes 4194304 | tf_op jit(solution)/shard_map/all_to_all | solution.py:32
  165.0 9.7 %fusion.14 = f32[96,64,256]{2,1,0:T(8,128)} fusion(bf16[96,256,256]{2,1,0:T(8,128)(2,1)} %param.10, bf16[96,256,64]{1,2,0:T(8,128)(2,1)S(1)} %gather_fusion, pred[96]{0:T(512)(128)(4,1)S(1)} %get-tuple-element.6), kind=kOutput, calls=%fused_computation.19 | convolution fusion | flops 806879232 | bytes 22020192 | tf_op jit(solution)/shard_map/sji,sjv->siv/dot_general | solution.py:82
  174.7 14.9 %fusion.27 = f32[96,256,64]{1,2,0:T(8,128)} fusion(bf16[96,256,256]{2,1,0:T(8,128)(2,1)} %param.10, f32[96,64,256]{2,1,0:T(8,128)} %fusion.14, bf16[96,256,64]{1,2,0:T(8,128)(2,1)} %param.8, f32[96]{0:T(128)S(1)} %get-tuple-element.7, f32[96,256]{1,0:T(8,128)S(1)} %copy-done), kind=kOutput, calls=%fused_computation.30 | convolution fusion | flops 822607872 | bytes 28410240 | tf_op jit(solution)/shard_map/sij,sjv->siv/dot_general | solution.py:73
  189.6 8.3 %copy.30 = f32[96,256,64]{0,2,1:T(8,128)} copy(f32[96,256,64]{1,2,0:T(8,128)} %fusion.27) | data formatting | bytes 12582912 | tf_op jit(solution)/shard_map/sij,sjv->siv/dot_general | solution.py:73
  197.9 10.6 %fusion.38 = f32[64,16384]{1,0:T(8,128)} fusion(f32[96,16384]{0,1:T(8,128)} %bitcast.78, s32[96]{0:T(128)S(1)} %copy-done.1), kind=kOutput, calls=%fused_computation.44 | convolution fusion | flops 1207965696 | bytes 10486144 | tf_op jit(solution)/shard_map/dot_general | solution.py:74
  208.5 7.4 %reshape_reshape.7 = f32[8,16,128,64]{3,2,1,0:T(8,128)} reshape(f32[64,16384]{1,0:T(8,128)} %fusion.38) | data formatting | bytes 8388608 | tf_op jit(solution)/shard_map/reshape;reshape | solution.py:58
  215.9 6.8 %copy.31 = f32[16,8,128,64]{2,3,1,0:T(8,128)} copy(f32[16,8,128,64]{3,2,0,1:T(8,128)} %bitcast.80) | data formatting | bytes 8388608 | tf_op jit(solution)/shard_map/transpose | solution.py:59
  225.2 8.3 %all_to_all.65 = f32[2,64,128,64]{2,3,1,0:T(8,128)} all-to-all(f32[2,64,128,64]{2,3,1,0:T(8,128)S(1)} %copy.32), channel_id=1, replica_groups=mesh['row_0'=4,'row_1'=4,'col_0'=4,'col_1'=2] {'col_1'}, dimensions={0} | all-to-all | bytes 8388608 | tf_op jit(solution)/shard_map/all_to_all | solution.py:20
  236.3 34.8 %all_to_all.66 = f32[64,128,64]{1,2,0:T(8,128)} all-to-all(f32[64,128,64]{1,2,0:T(8,128)S(1)} %reduce_sum.57), channel_id=1, replica_groups=mesh['row_0'=4,'row_1'=4,'col_0'=4,'col_1'=2] {'row_0','row_1','col_0'}, dimensions={0} | all-to-all | bytes 4194304 | tf_op jit(solution)/shard_map/all_to_all | solution.py:27
  272.8 9.9 %all_to_all.67 = bf16[16,128,64]{1,2,0:T(8,128)(2,1)S(1)} all-to-all(bf16[16,128,64]{1,2,0:T(8,128)(2,1)S(1)} %broadcast_in_dim.24), channel_id=1, replica_groups=mesh['row_0'=4,'row_1'=4,'col_0'=4,'col_1'=2] {'row_0','row_1'}, dimensions={0} | all-to-all | bytes 524288 | tf_op jit(solution)/shard_map/all_to_all | solution.py:32
  286.4 11.5 %all_to_all.68 = f32[8,128,64]{1,2,0:T(8,128)S(1)} all-to-all(f32[8,128,64]{1,2,0:T(8,128)S(1)} %bitcast.84), channel_id=1, replica_groups=mesh['row_0'=4,'row_1'=4,'col_0'=4,'col_1'=2] {'col_0','col_1'}, dimensions={0} | all-to-all | bytes 524288 | tf_op jit(solution)/shard_map/all_to_all | solution.py:20
  298.2 22.1 %all_to_all.69 = bf16[64,128,64]{1,2,0:T(8,128)(2,1)S(1)} all-to-all(bf16[64,128,64]{1,2,0:T(8,128)(2,1)S(1)} %broadcast_in_dim.25), channel_id=1, replica_groups=mesh['row_0'=4,'row_1'=4,'col_0'=4,'col_1'=2] {'row_0','row_1','col_0'}, dimensions={0} | all-to-all | bytes 2097152 | tf_op jit(solution)/shard_map/all_to_all | solution.py:32
  320.8 7.5 %all_to_all.70 = bf16[2,64,128,64]{2,3,1,0:T(8,128)(2,1)S(1)} all-to-all(bf16[2,64,128,64]{2,3,1,0:T(8,128)(2,1)S(1)} %broadcast_in_dim.26), channel_id=1, replica_groups=mesh['row_0'=4,'row_1'=4,'col_0'=4,'col_1'=2] {'col_1'}, dimensions={0} | all-to-all | bytes 4194304 | tf_op jit(solution)/shard_map/all_to_all | solution.py:32
  331.4 13.7 %fusion.3 = bf16[96,256,64]{1,2,0:T(8,128)(2,1)} fusion(f32[96,64,256]{2,1,0:T(8,128)} %fusion.14, bf16[96,256,64]{1,2,0:T(8,128)(2,1)} %param.8, f32[96]{0:T(128)S(1)} %get-tuple-element.7, f32[96,256]{1,0:T(8,128)S(1)} %copy-done, bf16[96,256,256]{2,1,0:T(8,128)(2,1)} %param.10, bf16[96,256,64]{1,2,0:T(8,128)(2,1)} %gather_fusion.1, ...), kind=kOutput, calls=%fused_computation.7 | convolution fusion | flops 836763648 | bytes 28410336 | tf_op jit(solution)/shard_map/sji,sjv->siv/dot_general | solution.py:82
  (30 shorter events, 36.6 us)
Async XLA Ops:
  13.5 8.4 %copy-start.1 = (s32[96]{0:T(128)S(1)}, s32[96]{0:T(128)}, u32[]{:S(2)}) copy-start(s32[96]{0:T(128)} %param.12) | copy-start | bytes 1156
  130.5 22.3 %all-to-all-start.4 = ((bf16[64,128,64]{1,2,0:T(8,128)(2,1)}), bf16[64,128,64]{1,2,0:T(8,128)(2,1)S(1)}, u32[]{:S(2)}, u32[]{:S(2)}) async-start(bf16[64,128,64]{1,2,0:T(8,128)(2,1)} %broadcast_in_dim.22), calls=%async_computation.4 | async-start | bytes 2097152 | tf_op jit(solution)/shard_map/all_to_all | solution.py:32
  165.0 9.7 %copy-start = (f32[96,256]{1,0:T(8,128)S(1)}, f32[96,256]{1,0:T(8,128)}, u32[]{:S(2)}) copy-start(f32[96,256]{1,0:T(8,128)} %param.9) | copy-start | bytes 294916
where the time goes:
time: 347 us; the launch traced here: 345 us
  blocking collectives  174 us (50%)
  matrix products  78.7 us (23%)
  local copies, waits for them, and re-layouts  59.8 us (17%)
  waiting for transfers between devices  17.4 us (5%)
  other arithmetic  9.74 us (3%)
  starting transfers between devices  4.86 us (1%)
    all_to_all x2, blocking collectives, summed_rows(): return jnp.sum(lax.all_to_all(own, far, 0, 0, tiled=True), axis=0)  75 us
    all_to_all x5, blocking collectives, from_everyone(): lax.all_to_all(jnp.broadcast_to(array[None], (length, *array.shape)), axi...  57.2 us
    all_to_all x4, blocking collectives, summed_on_arrival(): lax.all_to_all(in_blocks(array, dim, length), axis, 0, 0, tiled=True)  41.6 us
    dot_general x2, matrix products, apply_hamiltonian(): jnp.einsum('sij,sjv->siv', blocks, xb, preferred_element_type=jnp.float32)  27.1 us
    dot_general x2, matrix products, apply_hamiltonian(): jnp.einsum('sji,sjv->siv', blocks, picked, preferred_element_type=jnp.flo...  23.4 us
    dot_general x2, matrix products, apply_hamiltonian(): jnp.dot(onehot, proj.reshape(slots, nbasis * nvecs), precision=lax.Precis...  21.1 us
    all_to_all x1, waiting for transfers between devices, from_everyone(): lax.all_to_all(jnp.broadcast_to(array[None], (length, *array.shape)), axi...  17.4 us
    dot_general x2, local copies, waits for them, and re-layouts, apply_hamiltonian(): jnp.einsum('sij,sjv->siv', blocks, xb, preferred_element_type=jnp.float32)  16.7 us
  transfers between devices with their start and end apart: 1, of which 1 were waited for; matrix products, arithmetic and copies ran while one was open for 0% of the time, Pallas kernels for 0%

commit v1 on v0

v1 whole, which is shorter than its diff:
```python
import functools

import jax
import jax.numpy as jnp
from jax import lax
from jax.experimental import pallas as pl
from jax.experimental.pallas import tpu as pltpu
from jax.sharding import PartitionSpec as P

MESH = pl.DeviceIdType.MESH
F32 = jnp.float32
BF16 = jnp.bfloat16
STEP = 8
X, Y, Z = 0, 1, 2
ORDERS = ((X, Y, Z), (Y, Z, X), (Z, X, Y), (X, Z, Y))
NT = (((1,), (1,)), ((), ()))


def position():
    r, c = lax.axis_index("row"), lax.axis_index("col")
    return (c // 2, r // 4, r % 4, c % 2)


def device(x, y, z, k):
    return (y * 4 + z, x * 2 + k)


def peer(here, dim, step):
    there = list(here)
    there[dim] = (there[dim] + step) % 4
    return device(*there)


def at_dim(dim, index, rank):
    return tuple(index if d == dim else slice(None) for d in range(rank))


def coarse_body(u_ref, k_hbm, w_ref, kv, core_in, s1, r1, s2, r2, s3, r3, ub, ul, pw, rw,
                k_sem, core_ss, core_rs, rs_ss, rs_rs, yz_ss, yz_rs, pr_ss, pr_rs, ag_ss, ag_rs, fin_ss, fin_rs):
    here = position()
    x, y, z, k = here
    me = (y * 4 + z) * 8 + x * 2 + k
    sibling = device(x, y, z, 1 - k)
    yz_steps = [(i // 4, i % 4) for i in range(1, 16)]
    yz_peers = [device(x, (y + a) % 4, (z + b) % 4, k) for a, b in yz_steps]
    xk_steps = [(i // 2, i % 2) for i in range(1, 8)]
    xk_peers = [device((x + a) % 4, y, z, (k + b) % 2) for a, b in xk_steps]

    load = pltpu.make_async_copy(k_hbm, kv, k_sem)
    load.start()

    barrier = pltpu.get_barrier_semaphore()
    for p in yz_peers + xk_peers:
        pl.semaphore_signal(barrier, inc=1, device_id=p, device_id_type=MESH)
    pl.semaphore_wait(barrier, 22)

    def send(src, dst, ss, rs, to):
        copy = pltpu.make_async_remote_copy(src_ref=src, dst_ref=dst, send_sem=ss, recv_sem=rs, device_id=to, device_id_type=MESH)
        copy.start()
        return copy

    waits = []
    core = [send(u_ref.at[:, 1 - k, :, :, g], core_in.at[g], core_ss.at[g], core_rs.at[g], sibling) for g in range(4)]
    first = []
    for g in range(4):
        core[g].wait_recv()
        for a in range(4):
            s1[g, a] = (u_ref[a, k, :, :, g].astype(F32) + core_in[g, a].astype(F32)).astype(BF16)
        d = ORDERS[g][0]
        first.append([send(s1.at[(g,) + at_dim(d, (here[d] + o) % 4, 3)], r1.at[g, o - 1], rs_ss.at[g, 0, o - 1], rs_rs.at[g, 0, o - 1], peer(here, d, o)) for o in (1, 2, 3)])
    second = []
    for g in range(4):
        d, e, f = ORDERS[g]
        for c in first[g]:
            c.wait_recv()
        own = s1[(g,) + at_dim(d, here[d], 3)]
        s2[g] = (own.astype(F32) + r1[g, 0].astype(F32) + r1[g, 1].astype(F32) + r1[g, 2].astype(F32)).astype(BF16)
        at = 0 if e < f else 1
        second.append([send(s2.at[(g,) + at_dim(at, (here[e] + o) % 4, 2)], r2.at[g, o - 1], rs_ss.at[g, 1, o - 1], rs_rs.at[g, 1, o - 1], peer(here, e, o)) for o in (1, 2, 3)])
    third = []
    for g in range(4):
        d, e, f = ORDERS[g]
        for c in second[g]:
            c.wait_recv()
        at = 0 if e < f else 1
        own = s2[(g,) + at_dim(at, here[e], 2)]
        s3[g] = (own.astype(F32) + r2[g, 0].astype(F32) + r2[g, 1].astype(F32) + r2[g, 2].astype(F32)).astype(BF16)
        third.append([send(s3.at[g, (here[f] + o) % 4], r3.at[g, o - 1], rs_ss.at[g, 2, o - 1], rs_rs.at[g, 2, o - 1], peer(here, f, o)) for o in (1, 2, 3)])
    for g in range(4):
        f = ORDERS[g][2]
        for c in third[g]:
            c.wait_recv()
        total = s3[g, here[f]].astype(F32) + r3[g, 0].astype(F32) + r3[g, 1].astype(F32) + r3[g, 2].astype(F32)
        ub[y, z, g] = total.astype(BF16)
    spread = [send(ub.at[y, z], ub.at[y, z], yz_ss.at[i], yz_rs.at[i], yz_peers[i]) for i in range(15)]
    for c in core:
        c.wait_send()
    for c in sum(first + second + third, []):
        c.wait_send()
    load.wait()
    for c in spread:
        c.wait()
    for q in range(16):
        for g in range(4):
            ul[g * 16 : g * 16 + 16, q * 128 : q * 128 + 128] = ub[q // 4, q % 4, g]
    for n in range(4):
        part = lax.dot_general(ul[...], kv[n * 256 : n * 256 + 256, :], NT, preferred_element_type=F32).astype(BF16)
        for h in range(2):
            for g in range(4):
                pw[n, h, g] = part[g * 16 : g * 16 + 16, h * 128 : h * 128 + 128]
    swap = [send(pw.at[(x + a) % 4, (k + b) % 2], rw.at[i], pr_ss.at[i], pr_rs.at[i], xk_peers[i]) for i, (a, b) in enumerate(xk_steps)]
    for c in swap:
        c.wait()
    total = pw[x, k].astype(F32)
    for i in range(7):
        total = total + rw[i].astype(F32)
    w_ref[y, z, x, k] = total.astype(BF16)

    def part_of(g, free):
        ix = [slice(None) if d in free else here[d] for d in range(3)]
        return w_ref.at[ix[1], ix[2], ix[0], k, g]

    stages = []
    for stage in range(3):
        now = []
        for g in range(4):
            order = ORDERS[g][::-1]
            if stage > 0:
                for c in stages[stage - 1][g]:
                    c.wait_recv()
            block = part_of(g, order[:stage])
            now.append([send(block, block, ag_ss.at[g, stage, o - 1], ag_rs.at[g, stage, o - 1], peer(here, order[stage], o)) for o in (1, 2, 3)])
        stages.append(now)
    last = []
    for g in range(4):
        for c in stages[2][g]:
            c.wait_recv()
        block = part_of(g, (X, Y, Z))
        last.append(send(block, block, fin_ss.at[g], fin_rs.at[g], sibling))
    for now in stages:
        for c in sum(now, []):
            c.wait_send()
    for c in last:
        c.wait()


def coarse(part, kernel):
    dma = pltpu.SemaphoreType.DMA
    whole = pl.pallas_call(
        coarse_body,
        name="coarse",
        out_shape=jax.ShapeDtypeStruct((4, 4, 4, 2, 4, 16, 128), BF16),
        in_specs=[pl.BlockSpec(memory_space=pltpu.VMEM), pl.BlockSpec(memory_space=pl.ANY)],
        out_specs=pl.BlockSpec(memory_space=pltpu.VMEM),
        scratch_shapes=[
            pltpu.VMEM(kernel.shape, BF16),
            pltpu.VMEM((4, 4, 4, 4, 16, 128), BF16),
            pltpu.VMEM((4, 4, 4, 4, 16, 128), BF16),
            pltpu.VMEM((4, 3, 4, 4, 16, 128), BF16),
            pltpu.VMEM((4, 4, 4, 16, 128), BF16),
            pltpu.VMEM((4, 3, 4, 16, 128), BF16),
            pltpu.VMEM((4, 4, 16, 128), BF16),
            pltpu.VMEM((4, 3, 16, 128), BF16),
            pltpu.VMEM((4, 4, 4, 16, 128), BF16),
            pltpu.VMEM((64, 2048), BF16),
            pltpu.VMEM((4, 2, 4, 16, 128), BF16),
            pltpu.VMEM((7, 4, 16, 128), BF16),
            dma, dma((4,)), dma((4,)), dma((4, 3, 3)), dma((4, 3, 3)), dma((15,)), dma((15,)), dma((7,)), dma((7,)),
            dma((4, 3, 3)), dma((4, 3, 3)), dma((4,)), dma((4,)),
        ],
        compiler_params=pltpu.CompilerParams(collective_id=0, has_side_effects=True, vmem_limit_bytes=40 << 20),
    )(part.reshape(4, 2, 4, 4, 4, 16, 128), kernel)
    return whole.reshape(64, 2, 64, 128)


def add_in(acc, points, slot, value):
    p = points[slot]
    acc[p, 0] += value[:, :128]
    acc[p, 1] += value[:, 128:]


def project_body(points, counts, v_ref, b_ref, u_ref, acc):
    step = pl.program_id(0)

    @pl.when(step == 0)
    def _():
        acc[...] = jnp.zeros_like(acc)

    for s in range(STEP):
        slot = step * STEP + s
        live = (slot < counts[0]).astype(BF16)
        value = lax.dot_general(v_ref[s] * live, b_ref[s], NT, preferred_element_type=F32)
        add_in(acc, points, slot, value)

    @pl.when(step == pl.num_programs(0) - 1)
    def _():
        u_ref[...] = acc[...].astype(BF16)


def back_of(points, slot, w_ref, b):
    p = points[slot]
    w = jnp.concatenate([w_ref[p, 0], w_ref[p, 1]], axis=1)
    return jnp.dot(w, b, preferred_element_type=F32)


def middle_body(points, counts, v_ref, e_ref, b_ref, w_ref, t_ref, u_ref, acc):
    step = pl.program_id(0)

    @pl.when(step == 0)
    def _():
        acc[...] = jnp.zeros_like(acc)

    for s in range(STEP):
        slot = step * STEP + s
        live = (slot < counts[0]).astype(F32)
        back = back_of(points, slot, w_ref, b_ref[s])
        start = v_ref[s].astype(F32)
        first = (((e_ref[s : s + 1] - 2.0) * start + back) * (0.5 * live)).astype(BF16)
        t_ref[s] = first
        value = lax.dot_general(first, b_ref[s], NT, preferred_element_type=F32)
        add_in(acc, points, slot, value)

    @pl.when(step == pl.num_programs(0) - 1)
    def _():
        u_ref[...] = acc[...].astype(BF16)


def final_body(points, counts, v_ref, e_ref, b_ref, w_ref, t_ref, o_ref):
    step = pl.program_id(0)
    for s in range(STEP):
        slot = step * STEP + s
        live = (slot < counts[0]).astype(F32)
        back = back_of(points, slot, w_ref, b_ref[s])
        second = (e_ref[s : s + 1] - 2.0) * t_ref[s].astype(F32) + (back - v_ref[s].astype(F32)) * live
        o_ref[s] = second.astype(BF16)


def fine_call(body, name, args, outs, acc):
    points, counts, *rest = args
    slots = points.shape[0]

    def spec(shape):
        if shape[0] == slots:
            zeros = (0,) * (len(shape) - 1)
            return pl.BlockSpec((STEP,) + shape[1:], lambda i, *_: (i,) + zeros)
        return pl.BlockSpec(shape, lambda i, *_: (0,) * len(shape))

    return pl.pallas_call(
        body,
        name=name,
        out_shape=outs,
        grid_spec=pltpu.PrefetchScalarGridSpec(
            num_scalar_prefetch=2,
            grid=(slots // STEP,),
            in_specs=[spec(a.shape) for a in rest],
            out_specs=jax.tree.map(lambda o: spec(o.shape), outs),
            scratch_shapes=[pltpu.VMEM((64, 2, 64, 128), F32)] if acc else [],
        ),
        compiler_params=pltpu.CompilerParams(dimension_semantics=("arbitrary",), vmem_limit_bytes=40 << 20),
    )(*args)


def local(vectors, energies, blocks, kernel, slot_coarse_kpoint, counts):
    v = vectors.transpose(0, 2, 1)
    coarse_shape = jax.ShapeDtypeStruct((64, 2, 64, 128), BF16)
    fine_shape = jax.ShapeDtypeStruct(v.shape, BF16)
    u = fine_call(project_body, "project", (slot_coarse_kpoint, counts, v, blocks), coarse_shape, True)
    w = coarse(u, kernel)
    t, u = fine_call(middle_body, "middle", (slot_coarse_kpoint, counts, v, energies, blocks, w), (fine_shape, coarse_shape), True)
    w = coarse(u, kernel)
    out = fine_call(final_body, "final", (slot_coarse_kpoint, counts, v, energies, blocks, w, t), fine_shape, False)
    return out.transpose(0, 2, 1)


def solution(mesh):
    both = ("row", "col")
    in_specs = (P(both, None, None), P(both, None), P(both, None, None), P("row", "col"), P(both), P(both))
    return jax.shard_map(local, mesh=mesh, in_specs=in_specs, out_specs=P(both, None, None), check_vma=False)
```

time: 347 us -> 145 us (0.42)
  blocking collectives: 174 us -> 0 us
  Pallas kernels: 0 us -> 141 us
  matrix products: 78.7 us -> 0 us
  local copies, waits for them, and re-layouts: 59.8 us -> 2.56 us
  waiting for transfers between devices: 17.4 us -> 0 us
  other arithmetic: 9.74 us -> 0 us
  starting transfers between devices: 4.86 us -> 0 us
    all_to_all x11 -> x0, blocking collectives: 174 us -> none  [the longest x2 75 us: summed_rows(): return jnp.sum(lax.all_to_all(own, far, 0, 0, tiled=True), axis=0)]
    pallas_call x0 -> x5, Pallas kernels: none -> 141 us  [the longest x2 102 us: coarse(): pl.pallas_call(coarse_body, name='coarse', out_shape=jax.ShapeDtypeStruct...]
    dot_general x8 -> x0, matrix products: 78.7 us -> none  [the longest x2 27.1 us: apply_hamiltonian(): jnp.einsum('sij,sjv->siv', blocks, xb, preferred_element_type=jnp.float32)]
    transpose x4 -> x0, local copies, waits for them, and re-layouts: 18.6 us -> none  [the longest x2 13.6 us: collect_coarse(): arranged = partial_value.reshape(n_col, n_row, piece, width).transpose(1,...]
    all_to_all x1 -> x0, waiting for transfers between devices: 17.4 us -> none  [from_everyone(): lax.all_to_all(jnp.broadcast_to(array[None], (length, *array.shape)), axi...]
    another operation x4 -> x0, local copies, waits for them, and re-layouts: 16.9 us -> none  [the longest x2 14.7 us: collect_coarse(): partial_value.reshape(n_col, n_row, piece, width).transpose(1, 0, 2, 3)]
    dot_general x2 -> x0, local copies, waits for them, and re-layouts: 16.7 us -> none  [apply_hamiltonian(): jnp.einsum('sij,sjv->siv', blocks, xb, preferred_element_type=jnp.float32)]
    reduce_sum x6 -> x0, other arithmetic: 9.07 us -> none  [the longest x4 5.6 us: summed_on_arrival(): return jnp.sum(pieces, axis=0)]
  transfers between devices with their start and end apart: 1 -> 0, of which waited for: 1 -> 0; matrix products, arithmetic and copies ran while one was open for 0% -> 0% of each run, Pallas kernels for 0% -> 0%
where the time goes in v1:
time: 145 us; the launch traced here: 144 us
  Pallas kernels  141 us (97%)
  local copies, waits for them, and re-layouts  2.56 us (2%)
    pallas_call x2, Pallas kernels, coarse(): pl.pallas_call(coarse_body, name='coarse', out_shape=jax.ShapeDtypeStruct...  102 us
    pallas_call x3, Pallas kernels, fine_call(): pl.pallas_call(body, name=name, out_shape=outs, grid_spec=pltpu.PrefetchS...  38.6 us

profile of v1, /device:TPU:1, one launch (start us, length us, event | category | flops | bytes accessed | tf_op | source)
XLA Modules:
  0.0 143.9 jit_solution(18063603664441849504)
XLA Ops:
  0.7 0.0 copy-start
  0.7 1.9 %copy-done = bf16[96,256,64]{1,2,0:T(8,128)(2,1)S(1)} copy-done((bf16[96,256,64]{1,2,0:T(8,128)(2,1)S(1)}, bf16[96,256,64]{1,2,0:T(8,128)(2,1)}, u32[]{:S(2)}) %copy-start) | copy-done | bytes 3145752
  2.5 0.0 copy-start.4
  2.5 0.7 copy-done.4
  3.2 0.0 copy-start.2
  3.2 12.2 %project.1 = bf16[64,2,64,128]{3,2,1,0:T(8,128)(2,1)S(1)} custom-call(s32[96]{0:T(128)S(1)} %copy-done.4, s32[1]{0:T(128)S(6)} %copy.7.counts, bf16[96,64,256]{2,1,0:T(8,128)(2,1)S(1)} %bitcast.6, bf16[96,256,256]{2,1,0:T(8,128)(2,1)} %b_ref.5), custom_call_target="tpu_custom_call" | custom-call | tf_op jit(solution)/shard_map/project/pallas_call | solution.py:248
  15.4 0.0 copy-done.2
  15.4 0.0 copy-start.1
  15.4 0.0 copy-start.3
  15.4 53.4 %coarse.2 = bf16[4,4,4,2,4,16,128]{6,5,4,3,2,1,0:T(8,128)(2,1)S(1)} custom-call(bf16[4,2,4,4,4,16,128]{6,5,4,3,2,1,0:T(8,128)(2,1)S(1)} %bitcast.11, bf16[1024,2048]{1,0:T(8,128)(2,1)S(1)} %copy-done.2), custom_call_target="tpu_custom_call" | custom-call | tf_op jit(solution)/shard_map/coarse/pallas_call | solution.py:149
  68.9 0.0 copy-done.1
  68.9 0.0 copy-done.3
  68.9 14.4 %middle.1 = (bf16[96,64,256]{2,1,0:T(8,128)(2,1)S(1)}, bf16[64,2,64,128]{3,2,1,0:T(8,128)(2,1)S(1)}) custom-call(s32[96]{0:T(128)S(1)} %copy-done.4, s32[1]{0:T(128)S(6)} %copy.7.counts, bf16[96,64,256]{2,1,0:T(8,128)(2,1)S(1)} %bitcast.7, f32[96,256]{1,0:T(8,128)S(1)} %copy-done.3, bf16[96,256,256]{2,1,0:T(8,128)(2,1)} %b_ref.5, ...), custom_call_target="tpu_custom_call" | custom-call | tf_op jit(solution)/shard_map/middle/pallas_call | solution.py:248
  83.3 48.6 %coarse.3 = bf16[4,4,4,2,4,16,128]{6,5,4,3,2,1,0:T(8,128)(2,1)S(1)} custom-call(bf16[4,2,4,4,4,16,128]{6,5,4,3,2,1,0:T(8,128)(2,1)S(1)} %bitcast.12, bf16[1024,2048]{1,0:T(8,128)(2,1)S(1)} %copy-done.2), custom_call_target="tpu_custom_call" | custom-call | tf_op jit(solution)/shard_map/coarse/pallas_call | solution.py:149
  131.8 12.0 %final.1 = bf16[96,64,256]{2,1,0:T(8,128)(2,1)} custom-call(s32[96]{0:T(128)S(1)} %copy-done.4, s32[1]{0:T(128)S(6)} %copy.7.counts, bf16[96,64,256]{2,1,0:T(8,128)(2,1)S(1)} %bitcast.8, f32[96,256]{1,0:T(8,128)S(1)} %copy-done.3, bf16[96,256,256]{2,1,0:T(8,128)(2,1)} %b_ref.5, bf16[64,2,64,128]{3,2,1,0:T(8,128)(2,1)S(1)} %bitcast.10, ...), custom_call_target="tpu_custom_call" | custom-call | tf_op jit(solution)/shard_map/final/pallas_call | solution.py:248
Async XLA Ops:
  0.7 1.9 %copy-start = (bf16[96,256,64]{1,2,0:T(8,128)(2,1)S(1)}, bf16[96,256,64]{1,2,0:T(8,128)(2,1)}, u32[]{:S(2)}) copy-start(bf16[96,256,64]{1,2,0:T(8,128)(2,1)} %param.6) | copy-start | bytes 9437188
  2.5 0.7 copy-start.4
  3.2 12.2 %copy-start.2 = (bf16[1024,2048]{1,0:T(8,128)(2,1)S(1)}, bf16[1024,2048]{1,0:T(8,128)(2,1)}, u32[]{:S(2)}) copy-start(bf16[1024,2048]{1,0:T(8,128)(2,1)} %k_hbm.3) | copy-start | bytes 12582916
  15.4 53.4 %copy-start.1 = (bf16[96,256,64]{1,2,0:T(8,128)(2,1)S(1)}, bf16[96,256,64]{1,2,0:T(8,128)(2,1)}, u32[]{:S(2)}) copy-start(bf16[96,256,64]{1,2,0:T(8,128)(2,1)} %param.6) | copy-start | bytes 9437188
  15.4 53.4 %copy-start.3 = (f32[96,256]{1,0:T(8,128)S(1)}, f32[96,256]{1,0:T(8,128)}, u32[]{:S(2)}) copy-start(f32[96,256]{1,0:T(8,128)} %e_ref.3) | copy-start | bytes 294916

commit v2 on v0

v2 whole, which is shorter than its diff:
```python
import functools

import jax
import jax.numpy as jnp
from jax import lax
from jax.experimental import pallas as pl
from jax.experimental.pallas import tpu as pltpu
from jax.sharding import PartitionSpec as P

MESH = pl.DeviceIdType.MESH
F32 = jnp.float32
BF16 = jnp.bfloat16
STEP = 8
FINE_VMEM = 26 << 20
X, Y, Z = 0, 1, 2
GROUPS = ((slice(0, 3), X, Y, Z), (slice(3, 6), Y, Z, X), (slice(6, 8), Z, X, Y))
FAR, NEAR = (2, 1, 3, 0), (0, 1, 3, 2)
STEPS = [(i, j) for i in NEAR for j in NEAR][1:]
NT = (((1,), (1,)), ((), ()))


def position():
    r, c = lax.axis_index("row"), lax.axis_index("col")
    return (c // 2, r // 4, r % 4, c % 2)


def device(x, y, z, k):
    return (y * 4 + z, x * 2 + k)


def coarse_body(u_ref, kv, w_ref, core_in, s1, r1, s2, r2, ub, ul, prod, pw, rw,
                core_ss, core_rs, big_ss, big_rs, pl_ss, pl_rs, yz_ss, yz_rs, pr_ss, pr_rs, ap_ss, ap_rs, ab_ss, ab_rs, fin_ss, fin_rs):
    here = position()
    x, y, z, k = here

    def peer(*moves):
        there = list(here)
        for dim, step in moves:
            there[dim] = (there[dim] + step) % (4 if dim < 3 else 2)
        return device(*there)

    def send(src, dst, ss, rs, to):
        copy = pltpu.make_async_remote_copy(src_ref=src, dst_ref=dst, send_sem=ss, recv_sem=rs, device_id=to, device_id_type=MESH)
        copy.start()
        return copy

    def natural(fixed):
        return tuple(fixed.get(d, slice(None)) for d in range(3))

    xk_steps = [(i // 2, i % 2) for i in range(1, 8)]
    near = [((d, o),) for d in range(3) for o in (1, 2, 3)]
    near += [((a, i), (b, j)) for a, b in ((X, Y), (Y, Z), (Z, X)) for i in (1, 2, 3) for j in (1, 2, 3)]
    near += [((3, 1),)] + [((X, o), (3, 1)) for o in (1, 2, 3)]
    barrier = pltpu.get_barrier_semaphore()
    for moves in near:
        pl.semaphore_signal(barrier, inc=1, device_id=peer(*moves), device_id_type=MESH)
    pl.semaphore_wait(barrier, len(near))

    sent = []
    core, big, plane = {}, {}, {}
    for r in FAR:
        for g, (v, c, a, b) in enumerate(GROUPS):
            ix = natural({a: (here[a] + r) % 4})
            core[g, r] = send(u_ref.at[ix[0], 1 - k, ix[1], ix[2], v], core_in.at[ix + (v,)], core_ss.at[g, r], core_rs.at[g, r], peer((3, 1)))
            sent.append(core[g, r])
    for r in FAR:
        for g, (v, c, a, b) in enumerate(GROUPS):
            row = (here[a] + r) % 4
            ix = natural({a: row})
            core[g, r].wait_recv()
            s1[ix + (v,)] = (u_ref[ix[0], k, ix[1], ix[2], v].astype(F32) + core_in[ix + (v,)].astype(F32)).astype(BF16)
            for o in (2, 1, 3):
                src = s1.at[natural({a: row, c: (here[c] + o) % 4}) + (v,)]
                dst = r1.at[g, o - 1, row, :, pl.ds(0, v.stop - v.start)]
                big[g, r, o] = send(src, dst, big_ss.at[g, r, o - 1], big_rs.at[g, r, o - 1], peer((c, o)))
                sent.append(big[g, r, o])
    for r in FAR:
        for g, (v, c, a, b) in enumerate(GROUPS):
            n = v.stop - v.start
            row = (here[a] + r) % 4
            for o in (1, 3, 2):
                big[g, r, o].wait_recv()
            total = s1[natural({a: row, c: here[c]}) + (v,)].astype(F32)
            for o in (1, 3, 2):
                total = total + r1[g, o - 1, row, :, :n].astype(F32)
            s2[g, row, :, :n] = total.astype(BF16)
            for j in FAR:
                if (r, j) != (0, 0):
                    i = STEPS.index((r, j))
                    plane[g, r, j] = send(s2.at[g, row, (here[b] + j) % 4, pl.ds(0, n)], r2.at[g, i, pl.ds(0, n)], pl_ss.at[g, i], pl_rs.at[g, i], peer((a, r), (b, j)))
                    sent.append(plane[g, r, j])
    for g, (v, c, a, b) in enumerate(GROUPS):
        n = v.stop - v.start
        total = s2[g, here[a], here[b], :n].astype(F32)
        for i, step in enumerate(STEPS):
            plane[(g,) + step].wait_recv()
            total = total + r2[g, i, :n].astype(F32)
        ub[y, z, v] = total.astype(BF16)
    spread = {}
    for i, (p, q) in enumerate(STEPS):
        spread[p, q] = send(ub.at[y, z], ub.at[y, z], yz_ss.at[i], yz_rs.at[i], peer((Y, p), (Z, q)))
        sent.append(spread[p, q])
    for first, r in enumerate(NEAR):
        row = (y + r) % 4
        for q in range(4):
            if (r, q) != (0, 0):
                spread[(-r) % 4, (-q) % 4].wait_recv()
        for q in range(4):
            ul[:, q * 128 : q * 128 + 128] = ub[row, q].reshape(64, 128)
        for n in range(4):
            rows = slice(n * 256, n * 256 + 256)
            part = lax.dot_general(ul[...], kv[rows, pl.ds(pl.multiple_of(row * 512, 512), 512)], NT, preferred_element_type=F32)
            prod[:, rows] = part if first == 0 else prod[:, rows] + part
    for n in range(8):
        pw[n // 2, n % 2] = prod[:, n * 128 : n * 128 + 128].astype(BF16).reshape(8, 8, 128)
    swap = [send(pw.at[(x + p) % 4, (k + q) % 2], rw.at[i], pr_ss.at[i], pr_rs.at[i], peer((X, p), (3, q))) for i, (p, q) in enumerate(xk_steps)]
    sent += swap
    total = pw[x, k].astype(F32)
    for i in range(7):
        swap[i].wait_recv()
        total = total + rw[i].astype(F32)
    w_ref[y, z, x, k] = total.astype(BF16)

    def part_of(v, fixed):
        ix = natural(fixed)
        return w_ref.at[ix[1], ix[2], ix[0], k, v]

    plane, big, last = {}, {}, []
    for i, (p, q) in enumerate(STEPS):
        for g, (v, c, a, b) in enumerate(GROUPS):
            block = part_of(v, {d: here[d] for d in range(3)})
            plane[g, p, q] = send(block, block, ap_ss.at[g, i], ap_rs.at[g, i], peer((a, p), (b, q)))
            sent.append(plane[g, p, q])
    for r in NEAR:
        for g, (v, c, a, b) in enumerate(GROUPS):
            for q in range(4):
                if (r, q) != (0, 0):
                    plane[g, (-r) % 4, (-q) % 4].wait_recv()
            block = part_of(v, {a: (here[a] + r) % 4, c: here[c]})
            for o in (2, 1, 3):
                big[g, r, o] = send(block, block, ab_ss.at[g, r, o - 1], ab_rs.at[g, r, o - 1], peer((c, o)))
                sent.append(big[g, r, o])
    for r in NEAR:
        for g, (v, c, a, b) in enumerate(GROUPS):
            for o in (1, 3, 2):
                big[g, r, o].wait_recv()
            block = part_of(v, {a: (here[a] + r) % 4})
            last.append(send(block, block, fin_ss.at[g, r], fin_rs.at[g, r], peer((3, 1))))
    for copy in last:
        copy.wait_recv()
    for copy in sent + last:
        copy.wait_send()


def coarse(part, kernel):
    dma = pltpu.SemaphoreType.DMA
    tile = (8, 128)
    whole = pl.pallas_call(
        coarse_body,
        name="coarse",
        out_shape=jax.ShapeDtypeStruct((4, 4, 4, 2, 8) + tile, BF16),
        in_specs=[pl.BlockSpec(memory_space=pltpu.VMEM)] * 2,
        out_specs=pl.BlockSpec(memory_space=pltpu.VMEM),
        scratch_shapes=[
            pltpu.VMEM((4, 4, 4, 8) + tile, BF16),
            pltpu.VMEM((4, 4, 4, 8) + tile, BF16),
            pltpu.VMEM((3, 3, 4, 4, 3) + tile, BF16),
            pltpu.VMEM((3, 4, 4, 3) + tile, BF16),
            pltpu.VMEM((3, 15, 3) + tile, BF16),
            pltpu.VMEM((4, 4, 8) + tile, BF16),
            pltpu.VMEM((64, 512), BF16),
            pltpu.VMEM((64, 1024), F32),
            pltpu.VMEM((4, 2, 8) + tile, BF16),
            pltpu.VMEM((7, 8) + tile, BF16),
        ]
        + [dma(s) for s in ((3, 4), (3, 4, 3), (3, 15), (15,), (7,), (3, 15), (3, 4, 3), (3, 4)) for _ in range(2)],
        compiler_params=pltpu.CompilerParams(collective_id=0, has_side_effects=True, vmem_limit_bytes=10 << 20),
    )(part.reshape((4, 2, 4, 4, 8) + tile), kernel)
    return whole.reshape(64, 2, 64, 128)


def add_in(acc, points, slot, value):
    p = points[slot]
    acc[p, 0] += value[:, :128]
    acc[p, 1] += value[:, 128:]


def back_of(points, slot, w_ref, b):
    p = points[slot]
    w = jnp.concatenate([w_ref[p, 0], w_ref[p, 1]], axis=1)
    return jnp.dot(w, b, preferred_element_type=F32)


def project_body(points, counts, v_hbm, b_hbm, u_ref, b_ref, acc, v_ref, v_sem, b_sem):
    def chunk(i):
        rows = pl.ds(i * STEP, STEP)
        return (
            pltpu.make_async_copy(v_hbm.at[rows], v_ref.at[rows], v_sem.at[i]),
            pltpu.make_async_copy(b_hbm.at[rows], b_ref.at[rows], b_sem.at[i]),
        )

    chunks = b_ref.shape[0] // STEP
    for i in range(chunks):
        for copy in chunk(i):
            copy.start()
    acc[...] = jnp.zeros_like(acc)

    @pl.loop(0, chunks)
    def _(i):
        for copy in chunk(i):
            copy.wait()
        for s in range(STEP):
            slot = i * STEP + s
            live = (slot < counts[0]).astype(BF16)
            value = lax.dot_general(v_ref[slot] * live, b_ref[slot], NT, preferred_element_type=F32)
            add_in(acc, points, slot, value)

    u_ref[...] = acc[...].astype(BF16)


def middle_body(points, counts, v_ref, e_ref, b_ref, w_ref, t_ref, u_ref, acc):
    acc[...] = jnp.zeros_like(acc)

    @pl.loop(0, b_ref.shape[0] // STEP)
    def _(i):
        gain = e_ref[pl.ds(pl.multiple_of(i * STEP, STEP), STEP)] - 2.0
        for s in range(STEP):
            slot = i * STEP + s
            live = (slot < counts[0]).astype(F32)
            back = back_of(points, slot, w_ref, b_ref[slot])
            start = v_ref[slot].astype(F32)
            first = ((gain[s : s + 1] * start + back) * (0.5 * live)).astype(BF16)
            t_ref[slot] = first
            value = lax.dot_general(first, b_ref[slot], NT, preferred_element_type=F32)
            add_in(acc, points, slot, value)

    u_ref[...] = acc[...].astype(BF16)


def final_body(points, counts, v_ref, e_ref, b_ref, w_ref, t_ref, o_hbm, o_ref, o_sem):
    def chunk(i):
        rows = pl.ds(i * STEP, STEP)
        return pltpu.make_async_copy(o_ref.at[rows], o_hbm.at[rows], o_sem.at[i])

    chunks = b_ref.shape[0] // STEP

    @pl.loop(0, chunks)
    def _(i):
        gain = e_ref[pl.ds(pl.multiple_of(i * STEP, STEP), STEP)] - 2.0
        for s in range(STEP):
            slot = i * STEP + s
            live = (slot < counts[0]).astype(F32)
            back = back_of(points, slot, w_ref, b_ref[slot])
            second = gain[s : s + 1] * t_ref[slot].astype(F32) + (back - v_ref[slot].astype(F32)) * live
            o_ref[slot] = second.astype(BF16)
        chunk(i).start()

    for i in range(chunks):
        chunk(i).wait()


def fine_call(body, name, args, outs, ins, out_specs, scratch):
    smem = pl.BlockSpec(memory_space=pltpu.SMEM)
    return pl.pallas_call(
        body,
        name=name,
        out_shape=outs,
        in_specs=[smem, smem] + ins,
        out_specs=out_specs,
        scratch_shapes=scratch,
        compiler_params=pltpu.CompilerParams(vmem_limit_bytes=FINE_VMEM),
    )(*args)


def local(vectors, energies, blocks, kernel, slot_coarse_kpoint, counts):
    v = vectors.transpose(0, 2, 1)
    chunks = v.shape[0] // STEP
    table = (slot_coarse_kpoint, counts)
    coarse_shape = jax.ShapeDtypeStruct((64, 2, 64, 128), BF16)
    fine_shape = jax.ShapeDtypeStruct(v.shape, BF16)
    block_shape = jax.ShapeDtypeStruct(blocks.shape, BF16)
    acc = pltpu.VMEM(coarse_shape.shape, F32)
    vmem = pl.BlockSpec(memory_space=pltpu.VMEM)
    dma = pltpu.SemaphoreType.DMA
    u, held = fine_call(project_body, "project", table + (v, blocks), (coarse_shape, block_shape), [pl.BlockSpec(memory_space=pltpu.HBM)] * 2, (vmem, vmem),
                        [acc, pltpu.VMEM(v.shape, BF16), dma((chunks,)), dma((chunks,))])
    w = coarse(u, kernel)
    t, u = fine_call(middle_body, "middle", table + (v, energies, held, w), (fine_shape, coarse_shape), [vmem] * 4, (vmem, vmem), [acc])
    w = coarse(u, kernel)
    out = fine_call(final_body, "final", table + (v, energies, held, w, t), fine_shape, [vmem] * 5, pl.BlockSpec(memory_space=pltpu.HBM),
                    [pltpu.VMEM(v.shape, BF16), dma((chunks,))])
    return out.transpose(0, 2, 1)


def solution(mesh):
    both = ("row", "col")
    in_specs = (P(both, None, None), P(both, None), P(both, None, None), P("row", "col"), P(both), P(both))
    return jax.shard_map(local, mesh=mesh, in_specs=in_specs, out_specs=P(both, None, None), check_vma=False)
```

time: 347 us -> 116 us (0.33)
  blocking collectives: 174 us -> 0 us
  Pallas kernels: 0 us -> 112 us
  matrix products: 78.7 us -> 0 us
  local copies, waits for them, and re-layouts: 59.8 us -> 2.55 us
  waiting for transfers between devices: 17.4 us -> 0 us
  other arithmetic: 9.74 us -> 0 us
  starting transfers between devices: 4.86 us -> 0 us
    all_to_all x11 -> x0, blocking collectives: 174 us -> none  [the longest x2 75 us: summed_rows(): return jnp.sum(lax.all_to_all(own, far, 0, 0, tiled=True), axis=0)]
    pallas_call x0 -> x5, Pallas kernels: none -> 112 us  [the longest x2 88.6 us: coarse(): pl.pallas_call(coarse_body, name='coarse', out_shape=jax.ShapeDtypeStruct...]
    dot_general x8 -> x0, matrix products: 78.7 us -> none  [the longest x2 27.1 us: apply_hamiltonian(): jnp.einsum('sij,sjv->siv', blocks, xb, preferred_element_type=jnp.float32)]
    transpose x4 -> x0, local copies, waits for them, and re-layouts: 18.6 us -> none  [the longest x2 13.6 us: collect_coarse(): arranged = partial_value.reshape(n_col, n_row, piece, width).transpose(1,...]
    all_to_all x1 -> x0, waiting for transfers between devices: 17.4 us -> none  [from_everyone(): lax.all_to_all(jnp.broadcast_to(array[None], (length, *array.shape)), axi...]
    another operation x4 -> x0, local copies, waits for them, and re-layouts: 16.9 us -> none  [the longest x2 14.7 us: collect_coarse(): partial_value.reshape(n_col, n_row, piece, width).transpose(1, 0, 2, 3)]
    dot_general x2 -> x0, local copies, waits for them, and re-layouts: 16.7 us -> none  [apply_hamiltonian(): jnp.einsum('sij,sjv->siv', blocks, xb, preferred_element_type=jnp.float32)]
    reduce_sum x6 -> x0, other arithmetic: 9.07 us -> none  [the longest x4 5.6 us: summed_on_arrival(): return jnp.sum(pieces, axis=0)]
  transfers between devices with their start and end apart: 1 -> 0, of which waited for: 1 -> 0; matrix products, arithmetic and copies ran while one was open for 0% -> 0% of each run, Pallas kernels for 0% -> 0%
where the time goes in v2:
time: 116 us; the launch traced here: 115 us
  Pallas kernels  112 us (97%)
  local copies, waits for them, and re-layouts  2.55 us (2%)
    pallas_call x2, Pallas kernels, coarse(): pl.pallas_call(coarse_body, name='coarse', out_shape=jax.ShapeDtypeStruct...  88.6 us
    pallas_call x3, Pallas kernels, fine_call(): pl.pallas_call(body, name=name, out_shape=outs, in_specs=[smem, smem] + i...  23.6 us
    unnamed x8, local copies, waits for them, and re-layouts  2.55 us

profile of v2, /device:TPU:1, one launch (start us, length us, event | category | flops | bytes accessed | tf_op | source)
XLA Modules:
  0.0 115.5 jit_solution(491263627437558897)
XLA Ops:
  0.7 0.0 copy-start
  0.7 1.9 %copy-done = bf16[96,256,64]{1,2,0:T(8,128)(2,1)S(1)} copy-done((bf16[96,256,64]{1,2,0:T(8,128)(2,1)S(1)}, bf16[96,256,64]{1,2,0:T(8,128)(2,1)}, u32[]{:S(2)}) %copy-start) | copy-done | bytes 3145752
  2.5 0.0 copy-start.3
  2.5 0.7 copy-done.3
  3.2 0.0 copy-start.1
  3.2 7.9 %project.1 = (bf16[64,2,64,128]{3,2,1,0:T(8,128)(2,1)S(1)}, bf16[96,256,256]{2,1,0:T(8,128)(2,1)S(1)}) custom-call(s32[96]{0:T(128)S(1)} %copy-done.3, s32[1]{0:T(128)S(6)} %copy.7.counts, bf16[96,64,256]{2,1,0:T(8,128)(2,1)S(1)} %bitcast.6, bf16[96,256,256]{2,1,0:T(8,128)(2,1)} %b_hbm.1), custom_call_target="tpu_custom_call" | custom-call | tf_op jit(solution)/shard_map/project/pallas_call | solution.py:264
  11.1 0.0 copy-done.1
  11.1 0.0 copy-start.2
  11.2 47.0 %coarse.2 = bf16[4,4,4,2,8,8,128]{6,5,4,3,2,1,0:T(8,128)(2,1)S(1)} custom-call(bf16[4,2,4,4,8,8,128]{6,5,4,3,2,1,0:T(8,128)(2,1)S(1)} %bitcast.12, bf16[1024,2048]{1,0:T(8,128)(2,1)S(1)} %copy-done.1), custom_call_target="tpu_custom_call" | custom-call | tf_op jit(solution)/shard_map/coarse/pallas_call | solution.py:158
  58.1 0.0 copy-done.2
  58.2 10.6 %middle.1 = (bf16[96,64,256]{2,1,0:T(8,128)(2,1)S(1)}, bf16[64,2,64,128]{3,2,1,0:T(8,128)(2,1)S(1)}) custom-call(s32[96]{0:T(128)S(1)} %copy-done.3, s32[1]{0:T(128)S(6)} %copy.7.counts, bf16[96,64,256]{2,1,0:T(8,128)(2,1)S(1)} %bitcast.7, f32[96,256]{1,0:T(8,128)S(1)} %copy-done.2, bf16[96,256,256]{2,1,0:T(8,128)(2,1)S(1)} %get-tuple-element.9.b_ref, ...), custom_call_target="tpu_custom_call" | custom-call | tf_op jit(solution)/shard_map/middle/pallas_call | solution.py:264
  68.8 41.6 %coarse.3 = bf16[4,4,4,2,8,8,128]{6,5,4,3,2,1,0:T(8,128)(2,1)S(1)} custom-call(bf16[4,2,4,4,8,8,128]{6,5,4,3,2,1,0:T(8,128)(2,1)S(1)} %bitcast.11, bf16[1024,2048]{1,0:T(8,128)(2,1)S(1)} %copy-done.1), custom_call_target="tpu_custom_call" | custom-call | tf_op jit(solution)/shard_map/coarse/pallas_call | solution.py:158
  110.4 5.0 %final.1 = bf16[96,64,256]{2,1,0:T(8,128)(2,1)} custom-call(s32[96]{0:T(128)S(1)} %copy-done.3, s32[1]{0:T(128)S(6)} %copy.7.counts, bf16[96,64,256]{2,1,0:T(8,128)(2,1)S(1)} %bitcast.8, f32[96,256]{1,0:T(8,128)S(1)} %copy-done.2, bf16[96,256,256]{2,1,0:T(8,128)(2,1)S(1)} %get-tuple-element.9.b_ref, bf16[64,2,64,128]{3,2,1,0:T(8,128)(2,1)S(1)} %bitcast.9, ...), custom_call_target="tpu_custom_call" | custom-call | tf_op jit(solution)/shard_map/final/pallas_call | solution.py:264
Async XLA Ops:
  0.7 1.9 %copy-start = (bf16[96,256,64]{1,2,0:T(8,128)(2,1)S(1)}, bf16[96,256,64]{1,2,0:T(8,128)(2,1)}, u32[]{:S(2)}) copy-start(bf16[96,256,64]{1,2,0:T(8,128)(2,1)} %param.6) | copy-start | bytes 9437188
  2.5 0.7 copy-start.3
  3.2 7.9 %copy-start.1 = (bf16[1024,2048]{1,0:T(8,128)(2,1)S(1)}, bf16[1024,2048]{1,0:T(8,128)(2,1)}, u32[]{:S(2)}) copy-start(bf16[1024,2048]{1,0:T(8,128)(2,1)} %kv.3) | copy-start | bytes 12582916
  11.1 47.0 %copy-start.2 = (f32[96,256]{1,0:T(8,128)S(1)}, f32[96,256]{1,0:T(8,128)}, u32[]{:S(2)}) copy-start(f32[96,256]{1,0:T(8,128)} %e_ref.3) | copy-start | bytes 294916

commit v3 on v2

v3 whole, which is shorter than its diff:
```python
import functools

import jax
import jax.numpy as jnp
from jax import lax
from jax.experimental import pallas as pl
from jax.experimental.pallas import tpu as pltpu
from jax.sharding import PartitionSpec as P

MESH = pl.DeviceIdType.MESH
F32 = jnp.float32
BF16 = jnp.bfloat16
STEP = 8
MAIN_VMEM = 22 << 20
FINAL_VMEM = 8 << 20
X, Y, Z = 0, 1, 2
GROUPS = ((slice(0, 3), X, Y, Z), (slice(3, 6), Y, Z, X), (slice(6, 8), Z, X, Y))
FAR, NEAR = (2, 1, 3, 0), (0, 1, 3, 2)
STEPS = [(i, j) for i in NEAR for j in NEAR][1:]
NT = (((1,), (1,)), ((), ()))


def position():
    r, c = lax.axis_index("row"), lax.axis_index("col")
    return (lax.div(c, 2), lax.div(r, 4), lax.rem(r, 4), lax.rem(c, 2))


def moved(here, moves):
    there = list(here)
    for dim, step in moves:
        there[dim] = 1 - there[dim] if dim == 3 else lax.rem(there[dim] + step, 4)
    return there


def device(here, moves):
    x, y, z, k = moved(here, moves)
    return (y * 4 + z, x * 2 + k)


def natural(fixed):
    return tuple(fixed.get(d, slice(None)) for d in range(3))


SIBLING = (3, 1)
XK = [((X, i),) if not q else ((X, i), SIBLING) if i else (SIBLING,) for i in range(4) for q in range(2)][1:]
PEERS = [((d, o),) for d in range(3) for o in (1, 2, 3)]
PEERS += [((a, i), (b, j)) for a, b in ((X, Y), (Y, Z), (Z, X)) for i in (1, 2, 3) for j in (1, 2, 3)]
PEERS += [(SIBLING,)] + [((X, o), SIBLING) for o in (1, 2, 3)]


def greet(here):
    barrier = pltpu.get_barrier_semaphore()
    for moves in PEERS:
        pl.semaphore_signal(barrier, inc=1, device_id=device(here, moves), device_id_type=MESH)


def greeted():
    pl.semaphore_wait(pltpu.get_barrier_semaphore(), len(PEERS))


def send(here, src, dst, ss, rs, moves):
    pltpu.make_async_remote_copy(src_ref=src, dst_ref=dst, send_sem=ss, recv_sem=rs, device_id=device(here, moves), device_id_type=MESH).start()


def landed(here, ref, rs):
    pltpu.make_async_remote_copy(src_ref=ref, dst_ref=ref, send_sem=rs, recv_sem=rs, device_id=device(here, (SIBLING,)), device_id_type=MESH).wait_recv()


def gone(here, ref, ss):
    pltpu.make_async_remote_copy(src_ref=ref, dst_ref=ref, send_sem=ss, recv_sem=ss, device_id=device(here, (SIBLING,)), device_id_type=MESH).wait_send()


def moves_of(*pairs):
    return tuple(p for p in pairs if p[1])


def coarse_round(here, u_ref, kv, w_ref, core_in, s1, r1, s2, r2, ub, ul, prod, pw, rw, sems):
    (core_ss, core_rs, big_ss, big_rs, pl_ss, pl_rs, yz_ss, yz_rs, pr_ss, pr_rs, ap_ss, ap_rs, ab_ss, ab_rs, fin_ss, fin_rs) = sems
    x, y, z, k = here
    along = [[moved(here, ((d, o),))[d] for o in range(4)] for d in range(3)]

    for r in FAR:
        for g, (v, c, a, b) in enumerate(GROUPS):
            ix = natural({a: along[a][r]})
            send(here, u_ref.at[ix[0], 1 - k, ix[1], ix[2], v], core_in.at[ix + (v,)], core_ss, core_rs.at[g, r], (SIBLING,))
    for r in FAR:
        for g, (v, c, a, b) in enumerate(GROUPS):
            ix = natural({a: along[a][r]})
            landed(here, core_in.at[ix + (v,)], core_rs.at[g, r])
            s1[ix + (v,)] = (u_ref[ix[0], k, ix[1], ix[2], v].astype(F32) + core_in[ix + (v,)].astype(F32)).astype(BF16)
            for o in (2, 1, 3):
                src = s1.at[natural({a: along[a][r], c: along[c][o]}) + (v,)]
                send(here, src, r1.at[o - 1, along[a][r], :, v], big_ss, big_rs.at[g, r], ((c, o),))
    for r in FAR:
        for g, (v, c, a, b) in enumerate(GROUPS):
            row = along[a][r]
            landed(here, r1.at[:, row, :, v], big_rs.at[g, r])
            total = s1[natural({a: row, c: here[c]}) + (v,)].astype(F32)
            for o in range(3):
                total = total + r1[o, row, :, v].astype(F32)
            s2[row, :, v] = total.astype(BF16)
            for j in FAR:
                if (r, j) != (0, 0):
                    send(here, s2.at[row, along[b][j], v], r2.at[STEPS.index((r, j)), v], pl_ss, pl_rs.at[g], moves_of((a, r), (b, j)))
    for g, (v, c, a, b) in enumerate(GROUPS):
        landed(here, r2.at[:, v], pl_rs.at[g])
        total = s2[here[a], here[b], v].astype(F32)
        for i in range(15):
            total = total + r2[i, v].astype(F32)
        ub[y, z, v] = total.astype(BF16)
    for p, q in STEPS:
        send(here, ub.at[y, z], ub.at[y, z], yz_ss, yz_rs.at[p], moves_of((Y, p), (Z, q)))
    for first, r in enumerate(NEAR):
        row = along[Y][r]
        landed(here, ub.at[row] if r else ub.at[row, pl.ds(0, 3)], yz_rs.at[(-r) % 4])
        for q in range(4):
            ul[:, q * 128 : q * 128 + 128] = ub[row, q].reshape(64, 128)
        for n in range(4):
            rows = slice(n * 256, n * 256 + 256)
            part = lax.dot_general(ul[...], kv[rows, pl.ds(pl.multiple_of(row * 512, 512), 512)], NT, preferred_element_type=F32)
            prod[:, rows] = part if first == 0 else prod[:, rows] + part
    for n in range(8):
        pw[n // 2, n % 2] = prod[:, n * 128 : n * 128 + 128].astype(BF16).reshape(8, 8, 128)
    for i, moves in enumerate(XK):
        there = moved(here, moves)
        send(here, pw.at[there[0], there[3]], rw.at[i], pr_ss, pr_rs, moves)
    landed(here, rw, pr_rs)
    total = pw[x, k].astype(F32)
    for i in range(7):
        total = total + rw[i].astype(F32)
    w_ref[y, z, x, k] = total.astype(BF16)

    def part_of(v, fixed):
        ix = natural(fixed)
        return w_ref.at[ix[1], ix[2], ix[0], k, v]

    for p, q in STEPS:
        for g, (v, c, a, b) in enumerate(GROUPS):
            block = part_of(v, {d: here[d] for d in range(3)})
            send(here, block, block, ap_ss, ap_rs.at[g, p], moves_of((a, p), (b, q)))
    some = pl.ds(0, 3)
    for r in NEAR:
        for g, (v, c, a, b) in enumerate(GROUPS):
            row = {a: along[a][r], c: here[c]}
            landed(here, part_of(v, row if r else row | {b: some}), ap_rs.at[g, (-r) % 4])
            block = part_of(v, row)
            for o in (2, 1, 3):
                send(here, block, block, ab_ss, ab_rs.at[g, r], ((c, o),))
    for r in NEAR:
        for g, (v, c, a, b) in enumerate(GROUPS):
            row = {a: along[a][r]}
            landed(here, part_of(v, row | {c: some}), ab_rs.at[g, r])
            block = part_of(v, row)
            send(here, block, block, fin_ss, fin_rs, (SIBLING,))
    landed(here, w_ref.at[:, :, :, 1 - k], fin_rs)
    gone(here, core_in, core_ss)
    gone(here, s1.at[some], big_ss)
    gone(here, r2, pl_ss)
    gone(here, r2, yz_ss)
    gone(here, rw, pr_ss)
    gone(here, r2, ap_ss)
    gone(here, w_ref.at[some, :, :, 0], ab_ss)
    gone(here, w_ref.at[:, :, :, 0], fin_ss)


ROUND = [
    pltpu.VMEM((4, 4, 4, 8, 8, 128), BF16),
    pltpu.VMEM((4, 4, 4, 8, 8, 128), BF16),
    pltpu.VMEM((3, 4, 4, 8, 8, 128), BF16),
    pltpu.VMEM((4, 4, 8, 8, 128), BF16),
    pltpu.VMEM((15, 8, 8, 128), BF16),
    pltpu.VMEM((4, 4, 8, 8, 128), BF16),
    pltpu.VMEM((64, 512), BF16),
    pltpu.VMEM((64, 1024), F32),
    pltpu.VMEM((4, 2, 8, 8, 128), BF16),
    pltpu.VMEM((7, 8, 8, 128), BF16),
]
SEMS = [pltpu.SemaphoreType.DMA(s) for n in ((3, 4), (3, 4), (3,), (4,), (), (3, 4), (3, 4), ()) for s in ((), n)]


def back_of(points, slot, w_ref, b):
    p = points[slot]
    w = jnp.concatenate([w_ref[p, 0], w_ref[p, 1]], axis=1)
    return jnp.dot(w, b, preferred_element_type=F32)


def main_body(points, counts, links, v_hbm, e_hbm, b_hbm, k_hbm, t_ref, b_ref, w_ref,
              v_ref, e_ref, kv, sums, u_ref, v_sem, b_sem, e_sem, k_sem, *scratch):
    here = position()
    slots = b_ref.shape[0]
    chunks = slots // STEP
    greet(here)

    def chunk(i):
        rows = pl.ds(i * STEP, STEP)
        return (
            pltpu.make_async_copy(v_hbm.at[rows], v_ref.at[rows], v_sem.at[i]),
            pltpu.make_async_copy(b_hbm.at[rows], b_ref.at[rows], b_sem.at[i]),
        )

    for i in range(chunks):
        for copy in chunk(i):
            copy.start()
    energies = pltpu.make_async_copy(e_hbm, e_ref, e_sem)
    energies.start()
    table = pltpu.make_async_copy(k_hbm, kv, k_sem)
    table.start()
    sums[0] = jnp.zeros(sums.shape[1:], F32)

    def gather():
        @pl.loop(0, 64, unroll=2)
        def _(p):
            value = sums[links[slots + p]].astype(BF16)
            u_ref[p, 0] = value[:, :128].reshape(8, 8, 128)
            u_ref[p, 1] = value[:, 128:].reshape(8, 8, 128)

    @pl.loop(0, chunks)
    def _(i):
        for copy in chunk(i):
            copy.wait()
        for s in range(STEP):
            slot = i * STEP + s
            live = (slot < counts[0]).astype(BF16)
            value = lax.dot_general(v_ref[slot] * live, b_ref[slot], NT, preferred_element_type=F32)
            sums[slot + 1] = value + sums[links[slot]]

    gather()
    energies.wait()
    table.wait()
    greeted()
    u_view = u_ref.reshape(4, 2, 4, 4, 8, 8, 128)
    round_of = lambda: coarse_round(here, u_view, kv, w_ref, *scratch[: len(ROUND)], scratch[len(ROUND) :])
    round_of()
    w_view = w_ref.reshape(64, 2, 64, 128)

    @pl.loop(0, chunks)
    def _(i):
        gain = e_ref[pl.ds(pl.multiple_of(i * STEP, STEP), STEP)] - 2.0
        for s in range(STEP):
            slot = i * STEP + s
            live = (slot < counts[0]).astype(F32)
            back = back_of(points, slot, w_view, b_ref[slot])
            start = v_ref[slot].astype(F32)
            first = ((gain[s : s + 1] * start + back) * (0.5 * live)).astype(BF16)
            t_ref[slot] = first
            value = lax.dot_general(first, b_ref[slot], NT, preferred_element_type=F32)
            sums[slot + 1] = value + sums[links[slot]]

    gather()
    round_of()


def final_body(points, counts, v_ref, e_ref, b_ref, w_ref, t_ref, o_hbm, o_ref, o_sem):
    def chunk(i):
        rows = pl.ds(i * STEP, STEP)
        return pltpu.make_async_copy(o_ref.at[rows], o_hbm.at[rows], o_sem.at[i])

    chunks = b_ref.shape[0] // STEP

    @pl.loop(0, chunks)
    def _(i):
        gain = e_ref[pl.ds(pl.multiple_of(i * STEP, STEP), STEP)] - 2.0
        for s in range(STEP):
            slot = i * STEP + s
            live = (slot < counts[0]).astype(F32)
            back = back_of(points, slot, w_ref, b_ref[slot])
            second = gain[s : s + 1] * t_ref[slot].astype(F32) + (back - v_ref[slot].astype(F32)) * live
            o_ref[slot] = second.astype(BF16)
        chunk(i).start()

    for i in range(chunks):
        chunk(i).wait()


def local(vectors, energies, blocks, kernel, slot_coarse_kpoint, counts):
    v = vectors.transpose(0, 2, 1)
    slots = v.shape[0]
    chunks = slots // STEP
    query = lax.broadcasted_iota(jnp.int32, (slots + 64, slots), 0)
    order = lax.broadcasted_iota(jnp.int32, (slots + 64, slots), 1)
    point = jnp.pad(slot_coarse_kpoint, (0, 64))[:, None] + jnp.maximum(query - slots, 0)
    match = (point == slot_coarse_kpoint[None, :]) & (order < query)
    links = jnp.max(jnp.where(match, order + 1, 0), axis=1)
    coarse_shape = jax.ShapeDtypeStruct((4, 4, 4, 2, 8, 8, 128), BF16)
    fine_shape = jax.ShapeDtypeStruct(v.shape, BF16)
    block_shape = jax.ShapeDtypeStruct(blocks.shape, BF16)
    smem, vmem, hbm = (pl.BlockSpec(memory_space=m) for m in (pltpu.SMEM, pltpu.VMEM, pltpu.HBM))
    dma = pltpu.SemaphoreType.DMA
    t, held, w = pl.pallas_call(
        main_body,
        name="main",
        out_shape=(fine_shape, block_shape, coarse_shape),
        in_specs=[smem] * 3 + [hbm] * 4,
        out_specs=(vmem, vmem, vmem),
        scratch_shapes=[
            pltpu.VMEM(v.shape, BF16),
            pltpu.VMEM(energies.shape, F32),
            pltpu.VMEM(kernel.shape, BF16),
            pltpu.VMEM((slots + 1, 64, 256), F32),
            pltpu.VMEM((64, 2, 8, 8, 128), BF16),
            dma((chunks,)), dma((chunks,)), dma, dma,
        ] + ROUND + SEMS,
        compiler_params=pltpu.CompilerParams(collective_id=0, has_side_effects=True, vmem_limit_bytes=MAIN_VMEM),
    )(slot_coarse_kpoint, counts, links, *(pltpu.with_memory_space_constraint(a, pltpu.HBM) for a in (v, energies, blocks, kernel)))
    out = pl.pallas_call(
        final_body,
        name="final",
        out_shape=fine_shape,
        in_specs=[smem] * 2 + [vmem] * 5,
        out_specs=hbm,
        scratch_shapes=[pltpu.VMEM(v.shape, BF16), dma((chunks,))],
        compiler_params=pltpu.CompilerParams(vmem_limit_bytes=FINAL_VMEM),
    )(slot_coarse_kpoint, counts, v, energies, held, w.reshape(64, 2, 64, 128), t)
    return out.transpose(0, 2, 1)


def solution(mesh):
    both = ("row", "col")
    in_specs = (P(both, None, None), P(both, None), P(both, None, None), P("row", "col"), P(both), P(both))
    return jax.shard_map(local, mesh=mesh, in_specs=in_specs, out_specs=P(both, None, None), check_vma=False)
```

time: 116 us -> 100 us (0.86)
  Pallas kernels: 112 us -> 97.2 us
  local copies, waits for them, and re-layouts: 2.55 us -> 0.66 us
  other arithmetic: 0 us -> 1.5 us
    pallas_call x5 -> x2, Pallas kernels: 112 us -> 97.2 us  [the longest x1 92.1 us: local(): pl.pallas_call(main_body, name='main', out_shape=(fine_shape, block_shape...]
    unnamed x8 -> x6, local copies, waits for them, and re-layouts: 2.55 us -> 0.66 us
where the time goes in v3:
time: 100 us
  Pallas kernels  97.2 us (97%)
  other arithmetic  1.5 us (2%)
    pallas_call x1, Pallas kernels, local(): pl.pallas_call(main_body, name='main', out_shape=(fine_shape, block_shape...  92.1 us
    pallas_call x1, Pallas kernels, local(): pl.pallas_call(final_body, name='final', out_shape=fine_shape, in_specs=[...  5.05 us

profile of v3, /device:TPU:1, one launch (start us, length us, event | category | flops | bytes accessed | tf_op | source)
XLA Modules:
  0.0 100.0 jit_solution(6617095412287285333)
XLA Ops:
  0.7 0.7 maximum_add_fusion
  1.3 0.8 select_reduce_fusion.links
  2.2 0.0 copy-start.2
  2.2 0.6 copy-done.2
  2.8 0.0 copy-start
  2.8 0.0 copy-start.1
  2.8 92.1 %main.1 = (bf16[96,64,256]{2,1,0:T(8,128)(2,1)S(1)}, bf16[96,256,256]{2,1,0:T(8,128)(2,1)S(1)}, bf16[4,4,4,2,8,8,128]{6,5,4,3,2,1,0:T(8,128)(2,1)S(1)}) custom-call(s32[96]{0:T(128)S(1)} %copy-done.2, s32[1]{0:T(128)S(6)} %copy.7.counts, s32[160]{0:T(256)S(1)} %select_reduce_fusion.links, bf16[96,64,256]{2,1,0:T(8,128)(2,1)} %bitcast.3, f32[96,256]{1,0:T(8,128)} %e_ref.1, ...), custom_call_target="tpu_custom_call" | custom-call | tf_op jit(solution)/shard_map/main/pallas_call | solution.py:289
  94.9 0.0 copy-done
  95.0 0.0 copy-done.1
  95.0 5.0 %final.1 = bf16[96,64,256]{2,1,0:T(8,128)(2,1)} custom-call(s32[96]{0:T(128)S(1)} %copy-done.2, s32[1]{0:T(128)S(6)} %copy.7.counts, bf16[96,64,256]{2,1,0:T(8,128)(2,1)S(1)} %bitcast.4, f32[96,256]{1,0:T(8,128)S(1)} %copy-done.1, bf16[96,256,256]{2,1,0:T(8,128)(2,1)S(1)} %get-tuple-element.8.b_ref, bf16[64,2,64,128]{3,2,1,0:T(8,128)(2,1)S(1)} %bitcast.5, ...), custom_call_target="tpu_custom_call" | custom-call | tf_op jit(solution)/shard_map/final/pallas_call | solution.py:305
  (1 shorter events, 0.0 us)
Async XLA Ops:
  2.2 0.7 copy-start.2
  2.8 92.1 %copy-start = (bf16[96,256,64]{1,2,0:T(8,128)(2,1)S(1)}, bf16[96,256,64]{1,2,0:T(8,128)(2,1)}, u32[]{:S(2)}) copy-start(bf16[96,256,64]{1,2,0:T(8,128)(2,1)} %param.6) | copy-start | bytes 9437188
  2.8 92.1 %copy-start.1 = (f32[96,256]{1,0:T(8,128)S(1)}, f32[96,256]{1,0:T(8,128)}, u32[]{:S(2)}) copy-start(f32[96,256]{1,0:T(8,128)} %e_ref.1) | copy-start | bytes 294916

commit v4 on v3

--- a/solution.py
+++ b/solution.py
@@ -10,7 +10,7 @@
 MESH = pl.DeviceIdType.MESH
 F32 = jnp.float32
 BF16 = jnp.bfloat16
-STEP = 8
+STEP, MIDDLE, FINAL = 16, 24, 32
 MAIN_VMEM = 22 << 20
 FINAL_VMEM = 8 << 20
 X, Y, Z = 0, 1, 2
@@ -42,7 +42,7 @@
 
 
 SIBLING = (3, 1)
-XK = [((X, i),) if not q else ((X, i), SIBLING) if i else (SIBLING,) for i in range(4) for q in range(2)][1:]
+XK = [((X, i),) * (i > 0) + (SIBLING,) * q for i in range(4) for q in range(2)][1:]
 PEERS = [((d, o),) for d in range(3) for o in (1, 2, 3)]
 PEERS += [((a, i), (b, j)) for a, b in ((X, Y), (Y, Z), (Z, X)) for i in (1, 2, 3) for j in (1, 2, 3)]
 PEERS += [(SIBLING,)] + [((X, o), SIBLING) for o in (1, 2, 3)]
@@ -74,7 +74,7 @@
     return tuple(p for p in pairs if p[1])
 
 
-def coarse_round(here, u_ref, kv, w_ref, core_in, s1, r1, s2, r2, ub, ul, prod, pw, rw, sems):
+def coarse_round(here, u_ref, own_half, kv, w_ref, core_in, s1, r1, s2, r2, ub, ul, prod, pw, rw, sems):
     (core_ss, core_rs, big_ss, big_rs, pl_ss, pl_rs, yz_ss, yz_rs, pr_ss, pr_rs, ap_ss, ap_rs, ab_ss, ab_rs, fin_ss, fin_rs) = sems
     x, y, z, k = here
     along = [[moved(here, ((d, o),))[d] for o in range(4)] for d in range(3)]
@@ -83,6 +83,7 @@
         for g, (v, c, a, b) in enumerate(GROUPS):
             ix = natural({a: along[a][r]})
             send(here, u_ref.at[ix[0], 1 - k, ix[1], ix[2], v], core_in.at[ix + (v,)], core_ss, core_rs.at[g, r], (SIBLING,))
+    own_half()
     for r in FAR:
         for g, (v, c, a, b) in enumerate(GROUPS):
             ix = natural({a: along[a][r]})
@@ -115,15 +116,20 @@
         landed(here, ub.at[row] if r else ub.at[row, pl.ds(0, 3)], yz_rs.at[(-r) % 4])
         for q in range(4):
             ul[:, q * 128 : q * 128 + 128] = ub[row, q].reshape(64, 128)
-        for n in range(4):
-            rows = slice(n * 256, n * 256 + 256)
+        for o in FAR:
+            n = along[X][o]
+            rows = pl.ds(pl.multiple_of(n * 256, 256), 256)
             part = lax.dot_general(ul[...], kv[rows, pl.ds(pl.multiple_of(row * 512, 512), 512)], NT, preferred_element_type=F32)
-            prod[:, rows] = part if first == 0 else prod[:, rows] + part
-    for n in range(8):
-        pw[n // 2, n % 2] = prod[:, n * 128 : n * 128 + 128].astype(BF16).reshape(8, 8, 128)
-    for i, moves in enumerate(XK):
-        there = moved(here, moves)
-        send(here, pw.at[there[0], there[3]], rw.at[i], pr_ss, pr_rs, moves)
+            part = part if first == 0 else prod[o] + part
+            if first < 3:
+                prod[o] = part
+                continue
+            for h in range(2):
+                pw[n, h] = part[:, h * 128 : h * 128 + 128].astype(BF16).reshape(8, 8, 128)
+            for i, moves in enumerate(XK):
+                if dict(moves).get(X, 0) == o:
+                    there = moved(here, moves)
+                    send(here, pw.at[there[0], there[3]], rw.at[i], pr_ss, pr_rs, moves)
     landed(here, rw, pr_rs)
     total = pw[x, k].astype(F32)
     for i in range(7):
@@ -153,6 +159,11 @@
             block = part_of(v, row)
             send(here, block, block, fin_ss, fin_rs, (SIBLING,))
     landed(here, w_ref.at[:, :, :, 1 - k], fin_rs)
+
+
+def coarse_sent(here, w_ref, core_in, s1, r1, s2, r2, ub, ul, prod, pw, rw, sems):
+    core_ss, big_ss, pl_ss, yz_ss, pr_ss, ap_ss, ab_ss, fin_ss = sems[::2]
+    some = pl.ds(0, 3)
     gone(here, core_in, core_ss)
     gone(here, s1.at[some], big_ss)
     gone(here, r2, pl_ss)
@@ -171,7 +182,7 @@
     pltpu.VMEM((15, 8, 8, 128), BF16),
     pltpu.VMEM((4, 4, 8, 8, 128), BF16),
     pltpu.VMEM((64, 512), BF16),
-    pltpu.VMEM((64, 1024), F32),
+    pltpu.VMEM((4, 64, 256), F32),
     pltpu.VMEM((4, 2, 8, 8, 128), BF16),
     pltpu.VMEM((7, 8, 8, 128), BF16),
 ]
@@ -184,7 +195,7 @@
     return jnp.dot(w, b, preferred_element_type=F32)
 
 
-def main_body(points, counts, links, v_hbm, e_hbm, b_hbm, k_hbm, t_ref, b_ref, w_ref,
+def main_body(links, v_hbm, e_hbm, b_hbm, k_hbm, t_ref, b_ref, w_ref,
               v_ref, e_ref, kv, sums, u_ref, v_sem, b_sem, e_sem, k_sem, *scratch):
     here = position()
     slots = b_ref.shape[0]
@@ -207,9 +218,12 @@
     table.start()
     sums[0] = jnp.zeros(sums.shape[1:], F32)
 
-    def gather():
-        @pl.loop(0, 64, unroll=2)
-        def _(p):
+    points, count = slots + 64, 2 * slots + 64
+
+    def gather(half):
+        @pl.loop(0, 32, unroll=2)
+        def _(i):
+            p = lax.div(i, 8) * 16 + half * 8 + lax.rem(i, 8)
             value = sums[links[slots + p]].astype(BF16)
             u_ref[p, 0] = value[:, :128].reshape(8, 8, 128)
             u_ref[p, 1] = value[:, 128:].reshape(8, 8, 128)
@@ -220,55 +234,58 @@
             copy.wait()
         for s in range(STEP):
             slot = i * STEP + s
-            live = (slot < counts[0]).astype(BF16)
+            live = (slot < links[count]).astype(BF16)
             value = lax.dot_general(v_ref[slot] * live, b_ref[slot], NT, preferred_element_type=F32)
             sums[slot + 1] = value + sums[links[slot]]
 
-    gather()
+    gather(1 - here[3])
     energies.wait()
     table.wait()
     greeted()
     u_view = u_ref.reshape(4, 2, 4, 4, 8, 8, 128)
-    round_of = lambda: coarse_round(here, u_view, kv, w_ref, *scratch[: len(ROUND)], scratch[len(ROUND) :])
-    round_of()
+    buffers, sems = scratch[: len(ROUND)], scratch[len(ROUND) :]
+    coarse_round(here, u_view, lambda: gather(here[3]), kv, w_ref, *buffers, sems)
     w_view = w_ref.reshape(64, 2, 64, 128)
 
-    @pl.loop(0, chunks)
+    @pl.loop(0, slots // MIDDLE)
     def _(i):
-        gain = e_ref[pl.ds(pl.multiple_of(i * STEP, STEP), STEP)] - 2.0
-        for s in range(STEP):
-            slot = i * STEP + s
-            live = (slot < counts[0]).astype(F32)
-            back = back_of(points, slot, w_view, b_ref[slot])
+        gain = e_ref[pl.ds(pl.multiple_of(i * MIDDLE, 8), MIDDLE)] - 2.0
+        for s in range(MIDDLE):
+            slot = i * MIDDLE + s
+            live = (slot < links[count]).astype(F32)
+            back = back_of(links, points + slot, w_view, b_ref[slot])
             start = v_ref[slot].astype(F32)
             first = ((gain[s : s + 1] * start + back) * (0.5 * live)).astype(BF16)
             t_ref[slot] = first
             value = lax.dot_general(first, b_ref[slot], NT, preferred_element_type=F32)
             sums[slot + 1] = value + sums[links[slot]]
 
-    gather()
-    round_of()
-
-
-def final_body(points, counts, v_ref, e_ref, b_ref, w_ref, t_ref, o_hbm, o_ref, o_sem):
+    coarse_sent(here, w_ref, *buffers, sems)
+    gather(1 - here[3])
+    coarse_round(here, u_view, lambda: gather(here[3]), kv, w_ref, *buffers, sems)
+    coarse_sent(here, w_ref, *buffers, sems)
+
+
+def final_body(links, v_ref, e_ref, b_ref, w_ref, t_ref, o_hbm, o_ref, o_sem):
+    slots = b_ref.shape[0]
+    points, count = slots + 64, 2 * slots + 64
+
     def chunk(i):
-        rows = pl.ds(i * STEP, STEP)
+        rows = pl.ds(i * FINAL, FINAL)
         return pltpu.make_async_copy(o_ref.at[rows], o_hbm.at[rows], o_sem.at[i])
 
-    chunks = b_ref.shape[0] // STEP
-
-    @pl.loop(0, chunks)
+    @pl.loop(0, slots // FINAL)
     def _(i):
-        gain = e_ref[pl.ds(pl.multiple_of(i * STEP, STEP), STEP)] - 2.0
-        for s in range(STEP):
-            slot = i * STEP + s
-            live = (slot < counts[0]).astype(F32)
-            back = back_of(points, slot, w_ref, b_ref[slot])
+        gain = e_ref[pl.ds(pl.multiple_of(i * FINAL, 8), FINAL)] - 2.0
+        for s in range(FINAL):
+            slot = i * FINAL + s
+            live = (slot < links[count]).astype(F32)
+            back = back_of(links, points + slot, w_ref, b_ref[slot])
             second = gain[s : s + 1] * t_ref[slot].astype(F32) + (back - v_ref[slot].astype(F32)) * live
             o_ref[slot] = second.astype(BF16)
         chunk(i).start()
 
-    for i in range(chunks):
+    for i in range(slots // FINAL):
         chunk(i).wait()
 
 
@@ -276,11 +293,13 @@
     v = vectors.transpose(0, 2, 1)
     slots = v.shape[0]
     chunks = slots // STEP
-    query = lax.broadcasted_iota(jnp.int32, (slots + 64, slots), 0)
-    order = lax.broadcasted_iota(jnp.int32, (slots + 64, slots), 1)
-    point = jnp.pad(slot_coarse_kpoint, (0, 64))[:, None] + jnp.maximum(query - slots, 0)
+    rows = 2 * slots + 65
+    query = lax.broadcasted_iota(jnp.int32, (rows, slots), 0)
+    order = lax.broadcasted_iota(jnp.int32, (rows, slots), 1)
+    point = jnp.pad(slot_coarse_kpoint, (0, rows - slots))[:, None] + jnp.maximum(query - slots, 0)
     match = (point == slot_coarse_kpoint[None, :]) & (order < query)
-    links = jnp.max(jnp.where(match, order + 1, 0), axis=1)
+    plain = jnp.where(query == rows - 1, counts[0], jnp.where(order == query - (slots + 64), slot_coarse_kpoint[None, :], 0))
+    links = jnp.max(jnp.where(query < slots + 64, jnp.where(match, order + 1, 0), plain), axis=1)
     coarse_shape = jax.ShapeDtypeStruct((4, 4, 4, 2, 8, 8, 128), BF16)
     fine_shape = jax.ShapeDtypeStruct(v.shape, BF16)
     block_shape = jax.ShapeDtypeStruct(blocks.shape, BF16)
@@ -290,7 +309,7 @@
         main_body,
         name="main",
         out_shape=(fine_shape, block_shape, coarse_shape),
-        in_specs=[smem] * 3 + [hbm] * 4,
+        in_specs=[smem] + [hbm] * 4,
         out_specs=(vmem, vmem, vmem),
         scratch_shapes=[
             pltpu.VMEM(v.shape, BF16),
@@ -301,16 +320,16 @@
             dma((chunks,)), dma((chunks,)), dma, dma,
         ] + ROUND + SEMS,
         compiler_params=pltpu.CompilerParams(collective_id=0, has_side_effects=True, vmem_limit_bytes=MAIN_VMEM),
-    )(slot_coarse_kpoint, counts, links, *(pltpu.with_memory_space_constraint(a, pltpu.HBM) for a in (v, energies, blocks, kernel)))
+    )(links, *(pltpu.with_memory_space_constraint(a, pltpu.HBM) for a in (v, energies, blocks, kernel)))
     out = pl.pallas_call(
         final_body,
         name="final",
         out_shape=fine_shape,
-        in_specs=[smem] * 2 + [vmem] * 5,
+        in_specs=[smem] + [vmem] * 5,
         out_specs=hbm,
-        scratch_shapes=[pltpu.VMEM(v.shape, BF16), dma((chunks,))],
+        scratch_shapes=[pltpu.VMEM(v.shape, BF16), dma((slots // FINAL,))],
         compiler_params=pltpu.CompilerParams(vmem_limit_bytes=FINAL_VMEM),
-    )(slot_coarse_kpoint, counts, v, energies, held, w.reshape(64, 2, 64, 128), t)
+    )(links, v, energies, held, w.reshape(64, 2, 64, 128), t)
     return out.transpose(0, 2, 1)
 
 

time: 100 us -> 96.5 us (0.965)
  Pallas kernels: 97.2 us -> 94 us
    pallas_call x1, Pallas kernels: 92.1 us -> 90 us  [local(): pl.pallas_call(main_body, name='main', out_shape=(fine_shape, block_shape...]
    pallas_call x1, Pallas kernels: 5.05 us -> 4.01 us  [local(): pl.pallas_call(final_body, name='final', out_shape=fine_shape, in_specs=[...]
where the time goes in v4:
time: 96.5 us; the launch traced here: 96.4 us
  Pallas kernels  94 us (97%)
  other arithmetic  1.62 us (2%)
    pallas_call x1, Pallas kernels, local(): pl.pallas_call(main_body, name='main', out_shape=(fine_shape, block_shape...  90 us
    pallas_call x1, Pallas kernels, local(): pl.pallas_call(final_body, name='final', out_shape=fine_shape, in_specs=[...  4.01 us

profile of v4, /device:TPU:1, one launch (start us, length us, event | category | flops | bytes accessed | tf_op | source)
XLA Modules:
  0.0 96.4 jit_solution(5334877438063223276)
XLA Ops:
  0.7 0.7 iota_add_fusion
  1.3 1.0 select_reduce_fusion.links
  2.3 0.0 copy-start
  2.3 0.0 copy-start.1
  2.3 90.0 %main.1 = (bf16[96,64,256]{2,1,0:T(8,128)(2,1)S(1)}, bf16[96,256,256]{2,1,0:T(8,128)(2,1)S(1)}, bf16[4,4,4,2,8,8,128]{6,5,4,3,2,1,0:T(8,128)(2,1)S(1)}) custom-call(s32[257]{0:T(512)S(1)} %select_reduce_fusion.links, bf16[96,64,256]{2,1,0:T(8,128)(2,1)} %bitcast.5, f32[96,256]{1,0:T(8,128)} %e_ref.1, bf16[96,256,256]{2,1,0:T(8,128)(2,1)} %b_hbm.1, ...), custom_call_target="tpu_custom_call" | custom-call | tf_op jit(solution)/shard_map/main/pallas_call | solution.py:308
  92.4 0.0 copy-done
  92.4 0.0 copy-done.1
  92.4 4.0 %final.1 = bf16[96,64,256]{2,1,0:T(8,128)(2,1)} custom-call(s32[257]{0:T(512)S(1)} %select_reduce_fusion.links, bf16[96,64,256]{2,1,0:T(8,128)(2,1)S(1)} %bitcast.6, f32[96,256]{1,0:T(8,128)S(1)} %copy-done.1, bf16[96,256,256]{2,1,0:T(8,128)(2,1)S(1)} %get-tuple-element.8.b_ref, bf16[64,2,64,128]{3,2,1,0:T(8,128)(2,1)S(1)} %bitcast.7, ...), custom_call_target="tpu_custom_call" | custom-call | tf_op jit(solution)/shard_map/final/pallas_call | solution.py:324
  (2 shorter events, 0.0 us)
Async XLA Ops:
  2.3 90.1 %copy-start = (bf16[96,256,64]{1,2,0:T(8,128)(2,1)S(1)}, bf16[96,256,64]{1,2,0:T(8,128)(2,1)}, u32[]{:S(2)}) copy-start(bf16[96,256,64]{1,2,0:T(8,128)(2,1)} %param.6) | copy-start | bytes 9437188
  2.3 90.1 %copy-start.1 = (f32[96,256]{1,0:T(8,128)S(1)}, f32[96,256]{1,0:T(8,128)}, u32[]{:S(2)}) copy-start(f32[96,256]{1,0:T(8,128)} %e_ref.1) | copy-start | bytes 294916

commit v5 on v4

--- a/solution.py
+++ b/solution.py
@@ -10,7 +10,7 @@
 MESH = pl.DeviceIdType.MESH
 F32 = jnp.float32
 BF16 = jnp.bfloat16
-STEP, MIDDLE, FINAL = 16, 24, 32
+STEP, MIDDLE, FINAL = 16, 48, 32
 MAIN_VMEM = 22 << 20
 FINAL_VMEM = 8 << 20
 X, Y, Z = 0, 1, 2
@@ -151,13 +151,14 @@
             landed(here, part_of(v, row if r else row | {b: some}), ap_rs.at[g, (-r) % 4])
             block = part_of(v, row)
             for o in (2, 1, 3):
-                send(here, block, block, ab_ss, ab_rs.at[g, r], ((c, o),))
+                send(here, block, block, ab_ss, ab_rs.at[g, r, o - 1], ((c, o),))
+            send(here, block, block, fin_ss, fin_rs, (SIBLING,))
     for r in NEAR:
         for g, (v, c, a, b) in enumerate(GROUPS):
-            row = {a: along[a][r]}
-            landed(here, part_of(v, row | {c: some}), ab_rs.at[g, r])
-            block = part_of(v, row)
-            send(here, block, block, fin_ss, fin_rs, (SIBLING,))
+            for o in (1, 3, 2):
+                block = part_of(v, {a: along[a][r], c: along[c][4 - o]})
+                landed(here, block, ab_rs.at[g, r, o - 1])
+                send(here, block, block, fin_ss, fin_rs, (SIBLING,))
     landed(here, w_ref.at[:, :, :, 1 - k], fin_rs)
 
 
@@ -186,7 +187,7 @@
     pltpu.VMEM((4, 2, 8, 8, 128), BF16),
     pltpu.VMEM((7, 8, 8, 128), BF16),
 ]
-SEMS = [pltpu.SemaphoreType.DMA(s) for n in ((3, 4), (3, 4), (3,), (4,), (), (3, 4), (3, 4), ()) for s in ((), n)]
+SEMS = [pltpu.SemaphoreType.DMA(s) for n in ((3, 4), (3, 4), (3,), (4,), (), (3, 4), (3, 4, 3), ()) for s in ((), n)]
 
 
 def back_of(points, slot, w_ref, b):
@@ -221,7 +222,7 @@
     points, count = slots + 64, 2 * slots + 64
 
     def gather(half):
-        @pl.loop(0, 32, unroll=2)
+        @pl.loop(0, 32, unroll=8)
         def _(i):
             p = lax.div(i, 8) * 16 + half * 8 + lax.rem(i, 8)
             value = sums[links[slots + p]].astype(BF16)

time: 96.5 us -> 96 us (level)
  no operation moved by 1% of the time
where the time goes in v5:
time: 96 us; the launch traced here: 95.8 us
  Pallas kernels  93.5 us (97%)
  other arithmetic  1.62 us (2%)
    pallas_call x1, Pallas kernels, local(): pl.pallas_call(main_body, name='main', out_shape=(fine_shape, block_shape...  89.5 us
    pallas_call x1, Pallas kernels, local(): pl.pallas_call(final_body, name='final', out_shape=fine_shape, in_specs=[...  4.01 us

profile of v5, /device:TPU:1, one launch (start us, length us, event | category | flops | bytes accessed | tf_op | source)
XLA Modules:
  0.0 95.8 jit_solution(9480096380890035873)
XLA Ops:
  0.7 0.7 iota_add_fusion
  1.3 1.0 select_reduce_fusion.links
  2.3 0.0 copy-start
  2.3 0.0 copy-start.1
  2.3 89.5 %main.1 = (bf16[96,64,256]{2,1,0:T(8,128)(2,1)S(1)}, bf16[96,256,256]{2,1,0:T(8,128)(2,1)S(1)}, bf16[4,4,4,2,8,8,128]{6,5,4,3,2,1,0:T(8,128)(2,1)S(1)}) custom-call(s32[257]{0:T(512)S(1)} %select_reduce_fusion.links, bf16[96,64,256]{2,1,0:T(8,128)(2,1)} %bitcast.5, f32[96,256]{1,0:T(8,128)} %e_ref.1, bf16[96,256,256]{2,1,0:T(8,128)(2,1)} %b_hbm.1, ...), custom_call_target="tpu_custom_call" | custom-call | tf_op jit(solution)/shard_map/main/pallas_call | solution.py:309
  91.8 0.0 copy-done
  91.8 0.0 copy-done.1
  91.8 4.0 %final.1 = bf16[96,64,256]{2,1,0:T(8,128)(2,1)} custom-call(s32[257]{0:T(512)S(1)} %select_reduce_fusion.links, bf16[96,64,256]{2,1,0:T(8,128)(2,1)S(1)} %bitcast.6, f32[96,256]{1,0:T(8,128)S(1)} %copy-done.1, bf16[96,256,256]{2,1,0:T(8,128)(2,1)S(1)} %get-tuple-element.8.b_ref, bf16[64,2,64,128]{3,2,1,0:T(8,128)(2,1)S(1)} %bitcast.7, ...), custom_call_target="tpu_custom_call" | custom-call | tf_op jit(solution)/shard_map/final/pallas_call | solution.py:325
  (2 shorter events, 0.0 us)
Async XLA Ops:
  2.3 89.5 %copy-start = (bf16[96,256,64]{1,2,0:T(8,128)(2,1)S(1)}, bf16[96,256,64]{1,2,0:T(8,128)(2,1)}, u32[]{:S(2)}) copy-start(bf16[96,256,64]{1,2,0:T(8,128)(2,1)} %param.6) | copy-start | bytes 9437188
  2.3 89.5 %copy-start.1 = (f32[96,256]{1,0:T(8,128)S(1)}, f32[96,256]{1,0:T(8,128)}, u32[]{:S(2)}) copy-start(f32[96,256]{1,0:T(8,128)} %e_ref.1) | copy-start | bytes 294916

commit v6 on v5

--- a/solution.py
+++ b/solution.py
@@ -190,8 +190,8 @@
 SEMS = [pltpu.SemaphoreType.DMA(s) for n in ((3, 4), (3, 4), (3,), (4,), (), (3, 4), (3, 4, 3), ()) for s in ((), n)]
 
 
-def back_of(points, slot, w_ref, b):
-    p = points[slot]
+def back_of(links, slot, w_ref, b):
+    p = links[2, slot]
     w = jnp.concatenate([w_ref[p, 0], w_ref[p, 1]], axis=1)
     return jnp.dot(w, b, preferred_element_type=F32)
 
@@ -219,13 +219,12 @@
     table.start()
     sums[0] = jnp.zeros(sums.shape[1:], F32)
 
-    points, count = slots + 64, 2 * slots + 64
 
     def gather(half):
         @pl.loop(0, 32, unroll=8)
         def _(i):
             p = lax.div(i, 8) * 16 + half * 8 + lax.rem(i, 8)
-            value = sums[links[slots + p]].astype(BF16)
+            value = sums[links[1, p]].astype(BF16)
             u_ref[p, 0] = value[:, :128].reshape(8, 8, 128)
             u_ref[p, 1] = value[:, 128:].reshape(8, 8, 128)
 
@@ -235,9 +234,9 @@
             copy.wait()
         for s in range(STEP):
             slot = i * STEP + s
-            live = (slot < links[count]).astype(BF16)
+            live = (slot < links[1, 64]).astype(BF16)
             value = lax.dot_general(v_ref[slot] * live, b_ref[slot], NT, preferred_element_type=F32)
-            sums[slot + 1] = value + sums[links[slot]]
+            sums[slot + 1] = value + sums[links[0, slot]]
 
     gather(1 - here[3])
     energies.wait()
@@ -253,13 +252,13 @@
         gain = e_ref[pl.ds(pl.multiple_of(i * MIDDLE, 8), MIDDLE)] - 2.0
         for s in range(MIDDLE):
             slot = i * MIDDLE + s
-            live = (slot < links[count]).astype(F32)
-            back = back_of(links, points + slot, w_view, b_ref[slot])
+            live = (slot < links[1, 64]).astype(F32)
+            back = back_of(links, slot, w_view, b_ref[slot])
             start = v_ref[slot].astype(F32)
             first = ((gain[s : s + 1] * start + back) * (0.5 * live)).astype(BF16)
             t_ref[slot] = first
             value = lax.dot_general(first, b_ref[slot], NT, preferred_element_type=F32)
-            sums[slot + 1] = value + sums[links[slot]]
+            sums[slot + 1] = value + sums[links[0, slot]]
 
     coarse_sent(here, w_ref, *buffers, sems)
     gather(1 - here[3])
@@ -269,7 +268,6 @@
 
 def final_body(links, v_ref, e_ref, b_ref, w_ref, t_ref, o_hbm, o_ref, o_sem):
     slots = b_ref.shape[0]
-    points, count = slots + 64, 2 * slots + 64
 
     def chunk(i):
         rows = pl.ds(i * FINAL, FINAL)
@@ -280,8 +278,8 @@
         gain = e_ref[pl.ds(pl.multiple_of(i * FINAL, 8), FINAL)] - 2.0
         for s in range(FINAL):
             slot = i * FINAL + s
-            live = (slot < links[count]).astype(F32)
-            back = back_of(links, points + slot, w_ref, b_ref[slot])
+            live = (slot < links[1, 64]).astype(F32)
+            back = back_of(links, slot, w_ref, b_ref[slot])
             second = gain[s : s + 1] * t_ref[slot].astype(F32) + (back - v_ref[slot].astype(F32)) * live
             o_ref[slot] = second.astype(BF16)
         chunk(i).start()
@@ -294,13 +292,12 @@
     v = vectors.transpose(0, 2, 1)
     slots = v.shape[0]
     chunks = slots // STEP
-    rows = 2 * slots + 65
-    query = lax.broadcasted_iota(jnp.int32, (rows, slots), 0)
-    order = lax.broadcasted_iota(jnp.int32, (rows, slots), 1)
-    point = jnp.pad(slot_coarse_kpoint, (0, rows - slots))[:, None] + jnp.maximum(query - slots, 0)
-    match = (point == slot_coarse_kpoint[None, :]) & (order < query)
-    plain = jnp.where(query == rows - 1, counts[0], jnp.where(order == query - (slots + 64), slot_coarse_kpoint[None, :], 0))
-    links = jnp.max(jnp.where(query < slots + 64, jnp.where(match, order + 1, 0), plain), axis=1)
+    kind, query, order = (lax.broadcasted_iota(jnp.int32, (3, slots, slots), d) for d in range(3))
+    here, there = slot_coarse_kpoint[None, :, None], slot_coarse_kpoint[None, None, :]
+    match = (jnp.where(kind == 0, here, query) == there) & ((order < query) | (kind == 1))
+    found = jnp.where(match, order + 1, 0)
+    found = jnp.where((kind == 1) & (query == 64), counts[0], found)
+    links = jnp.max(jnp.where(kind == 2, here, found), axis=2)
     coarse_shape = jax.ShapeDtypeStruct((4, 4, 4, 2, 8, 8, 128), BF16)
     fine_shape = jax.ShapeDtypeStruct(v.shape, BF16)
     block_shape = jax.ShapeDtypeStruct(blocks.shape, BF16)

time: 96 us -> 95.4 us (level)
  no operation moved by 1% of the time
where the time goes in v6:
time: 95.4 us; the launch traced here: 95.3 us
  Pallas kernels  93.6 us (98%)
  other arithmetic  0.99 us (1%)
    pallas_call x1, Pallas kernels, local(): pl.pallas_call(main_body, name='main', out_shape=(fine_shape, block_shape...  89.6 us
    pallas_call x1, Pallas kernels, local(): pl.pallas_call(final_body, name='final', out_shape=fine_shape, in_specs=[...  4.02 us

profile of v6, /device:TPU:1, one launch (start us, length us, event | category | flops | bytes accessed | tf_op | source)
XLA Modules:
  0.0 95.3 jit_solution(13162725658267730620)
XLA Ops:
  0.7 1.0 %select_reduce_fusion.links = s32[3,96]{1,0:T(4,128)S(1)} fusion(s32[96]{0:T(128)S(1)} %iota_add_fusion, s32[96]{0:T(128)} %param.10, s32[]{:T(128)} %bitcast.4, pred[3]{0:T(512)(128)(4,1)S(1)} %get-tuple-element.11, pred[3]{0:T(512)(128)(4,1)S(1)} %iota_compare_fusion.4, pred[96]{0:T(512)(128)(4,1)S(1)} %iota_compare_fusion.2, ...), kind=kLoop, calls=%fused_computation | loop fusion | flops 276192 | bytes 2029 | tf_op jit(solution)/shard_map/reduce_max | solution.py:300
  1.7 0.0 copy-start
  1.7 0.0 copy-start.1
  1.7 89.6 %main.1 = (bf16[96,64,256]{2,1,0:T(8,128)(2,1)S(1)}, bf16[96,256,256]{2,1,0:T(8,128)(2,1)S(1)}, bf16[4,4,4,2,8,8,128]{6,5,4,3,2,1,0:T(8,128)(2,1)S(1)}) custom-call(s32[3,96]{1,0:T(4,128)S(1)} %select_reduce_fusion.links, bf16[96,64,256]{2,1,0:T(8,128)(2,1)} %bitcast.5, f32[96,256]{1,0:T(8,128)} %e_ref.1, bf16[96,256,256]{2,1,0:T(8,128)(2,1)} %b_hbm.1, ...), custom_call_target="tpu_custom_call" | custom-call | tf_op jit(solution)/shard_map/main/pallas_call | solution.py:306
  91.3 0.0 copy-done
  91.3 0.0 copy-done.1
  91.3 4.0 %final.1 = bf16[96,64,256]{2,1,0:T(8,128)(2,1)} custom-call(s32[3,96]{1,0:T(4,128)S(1)} %select_reduce_fusion.links, bf16[96,64,256]{2,1,0:T(8,128)(2,1)S(1)} %bitcast.6, f32[96,256]{1,0:T(8,128)S(1)} %copy-done.1, bf16[96,256,256]{2,1,0:T(8,128)(2,1)S(1)} %get-tuple-element.8.b_ref, bf16[64,2,64,128]{3,2,1,0:T(8,128)(2,1)S(1)} %bitcast.7, ...), custom_call_target="tpu_custom_call" | custom-call | tf_op jit(solution)/shard_map/final/pallas_call | solution.py:322
  (4 shorter events, 0.0 us)
Async XLA Ops:
  1.7 89.6 %copy-start = (bf16[96,256,64]{1,2,0:T(8,128)(2,1)S(1)}, bf16[96,256,64]{1,2,0:T(8,128)(2,1)}, u32[]{:S(2)}) copy-start(bf16[96,256,64]{1,2,0:T(8,128)(2,1)} %param.6) | copy-start | bytes 9437188
  1.7 89.6 %copy-start.1 = (f32[96,256]{1,0:T(8,128)S(1)}, f32[96,256]{1,0:T(8,128)}, u32[]{:S(2)}) copy-start(f32[96,256]{1,0:T(8,128)} %e_ref.1) | copy-start | bytes 294916
